TPU v7x, 32 devices: a whole 2x2x4 slice. The times are simulated.
32 devices in a mesh: macro: 16 (over z, x, core), vox: 2 (over y).
Axes of the slice: x: 2, y: 2, z: 4, core: 2. Of those that a mesh axis runs over, the one named last changes fastest.
Arguments:
- displacement: float32 [3, 1024], P(None, 'macro'), may hold values from -1.2 to 1.2
- load: float32 [3, 1024], P(None, 'macro'), may hold values from -6 to 6
- conn: int32 [8, 1024], P(None, 'macro'), may hold values from 0 to 79
- halo_list: int32 [256], P('macro'), may hold values from 0 to 63
- grad_ops: float32 [3, 8, 1024], P(None, None, 'macro'), may hold values from -3 to 3
- volume: float32 [1024], P('macro'), may hold values from 0.5 to 2
- elastic_moduli: float32 [2, 1024], P(None, 'macro'), may hold values from 1 to 4
- plastic_mask: int32 [1024], P('macro'), may hold values from 0 to 1, as said below
- new_owner: int32 [1024], P('macro'), may hold values from -1 to 15, as said below
- state: float32 [7, 1024, 16, 256], P(None, 'macro', 'vox'), may hold values from -0.6 to 1, as said below
- micro_moduli: float32 [4, 16, 256], P(None, 'vox'), may hold values from 0.5 to 6
Outputs:
- residual: float32 [3, 1024], P(None, 'macro')
- moved_state: float32 [7, 384, 16, 256], P(None, 'macro', 'vox')
Inputs may be any that keep to these rules, and one draw needn't show every extreme that they name: `plastic_mask`: each group's 64 points hold at most 48 plastic ones, 384 in all. `new_owner`: -1 exactly at elastic points; every group becomes the owner of exactly 24 plastic points, at most 3 of them from any one group. `state`: component 6 is nonnegative.
All inputs are finite; a program needn't handle non-finite values.
Results may differ from a plain program's by a relative error of at most 0.0001.
Values sent between devices are 32-bit elements; how exact they have to be, the bound alone decides.
A program may use at most 64 MiB of HBM per device.

v0:
```python
import functools
import math

import jax
import jax.numpy as jnp
import numpy as np
from jax import lax
from jax.experimental import pallas as pl
from jax.experimental.pallas import tpu as pltpu
from jax.sharding import PartitionSpec as P

RECV_AGG = 24
PLASTIC_MAX = 48
VOX_SIDE = 16
VOX_PLANE = 256
SWEEPS = 4
HALF = VOX_SIDE // 2
LANES = 128

LAM_REF = 3.0
MU_REF = 3.0
FULL_PREC = lax.Precision.HIGHEST

ROOT = math.sqrt(0.5)
COS1 = math.cos(math.pi / 8)
COS3 = math.cos(3 * math.pi / 8)
PAIRS = [(i, j) for i in range(6) for j in range(i, 6)]


def shifted(block, axis, distance):
    devices = range(lax.axis_size(axis))
    route = [((i - distance) % len(devices), i) for i in devices]
    return lax.ppermute(block, axis, route)


def green_tables():
    line = np.arange(VOX_SIDE)
    signed = np.where(line < HALF, line, line - VOX_SIDE).astype(np.float64)
    freq = np.stack(np.meshgrid(signed, signed, signed, indexing="ij"))
    norm = np.sum(freq * freq, axis=0)
    inverse = np.where(norm > 0, 1.0 / np.maximum(norm, 1.0), 0.0)
    coupling = (LAM_REF + MU_REF) / (LAM_REF + 2.0 * MU_REF)
    spots = [(0, 0), (1, 1), (2, 2), (1, 2), (0, 2), (0, 1)]
    table = np.zeros((6, 6) + norm.shape)
    for j, (a, b) in enumerate(spots):
        tau = np.zeros((3, 3))
        tau[a, b] = tau[b, a] = 1.0
        trac = np.einsum("ij,jxyz->ixyz", tau, freq)
        along = np.sum(freq * trac, axis=0) * inverse
        wave = (trac - coupling * along * freq) * inverse / MU_REF
        for i, (c, d) in enumerate(spots):
            table[i, j] = 0.5 * (freq[c] * wave[d] + freq[d] * wave[c])
    back = -line % VOX_SIDE
    flipped = table[:, :, back][:, :, :, back][:, :, :, :, back]
    even = 0.5 * (table + flipped) / VOX_SIDE**3
    even[:, 3:] *= 0.5
    stacked = np.stack([even[i, j] for i, j in PAIRS])
    return stacked.reshape(len(PAIRS), VOX_SIDE, VOX_PLANE).astype(np.float32)


def plane_tables():
    plane = np.arange(VOX_PLANE)
    rows, cols = plane // VOX_SIDE, plane % VOX_SIDE
    phase = (rows[:, None] * rows[None, :] + cols[:, None] * cols[None, :]) % VOX_SIDE
    angle = phase * (2.0 * math.pi / VOX_SIDE)
    plus = jnp.asarray((np.cos(angle) + np.sin(angle)).astype(np.float32))
    minus = jnp.asarray((np.cos(angle) - np.sin(angle)).astype(np.float32))
    out = []
    for table in (plus, minus):
        high = table.astype(jnp.bfloat16)
        out += [high, (table - high.astype(jnp.float32)).astype(jnp.bfloat16)]
    return jnp.stack(out)


def cosine_line(a):
    sums = [None] + [a[x] + a[8 - x] for x in (1, 2, 3)]
    diffs = [None] + [a[x] - a[8 - x] for x in (1, 2, 3)]
    even0, odd0 = a[0] + a[8], a[0] - a[8]
    outer, inner = even0 + a[4], even0 - a[4]
    spread = sums[1] + sums[3]
    slant = ROOT * (sums[1] - sums[3])
    mid = ROOT * diffs[2]
    first = COS1 * diffs[1] + COS3 * diffs[3]
    second = COS3 * diffs[1] - COS1 * diffs[3]
    top, low = odd0 + mid, odd0 - mid
    core = outer + sums[2]
    return [
        core + spread,
        top + first,
        inner + slant,
        low + second,
        outer - sums[2],
        low - second,
        inner - slant,
        top - first,
        core - spread,
    ]


def sine_line(b):
    sums = [None] + [b[x] + b[8 - x] for x in (1, 2, 3)]
    diffs = [None] + [b[x] - b[8 - x] for x in (1, 2, 3)]
    slant = ROOT * (diffs[1] + diffs[3])
    mid = ROOT * sums[2]
    first = COS3 * sums[1] + COS1 * sums[3]
    second = COS1 * sums[1] - COS3 * sums[3]
    return [
        None,
        (first + mid) + b[4],
        slant + diffs[2],
        (second + mid) - b[4],
        diffs[1] - diffs[3],
        (second - mid) + b[4],
        slant - diffs[2],
        (first - mid) - b[4],
    ]


def split_dot(block, table_ref, first):
    high = block.astype(jnp.bfloat16)
    low = (block - high.astype(jnp.float32)).astype(jnp.bfloat16)
    dot = functools.partial(jnp.dot, preferred_element_type=jnp.float32)
    return dot(high, table_ref[first]) + (dot(high, table_ref[first + 1]) + dot(low, table_ref[first]))


def voxel_law(strain, state, props, row):
    lam, mu = props[0, row, :], props[1, row, :]
    yield_base, harden = props[2, row, :], props[3, row, :]
    two_mu, three_mu = 2.0 * mu, 3.0 * mu
    stiff_inv = 1.0 / (three_mu + harden)
    bulk = lam + two_mu * (1.0 / 3.0)
    elastic = [strain[c] - state[c] for c in range(6)]
    trace = elastic[0] + elastic[1] + elastic[2]
    third = trace * (1.0 / 3.0)
    shape = [elastic[c] - third for c in range(3)] + elastic[3:]
    normal = shape[0] * shape[0] + shape[1] * shape[1] + shape[2] * shape[2]
    shear = shape[3] * shape[3] + shape[4] * shape[4] + shape[5] * shape[5]
    equivalent = two_mu * jnp.sqrt(1.5 * (normal + 2.0 * shear))
    strength = yield_base + harden * state[6]
    gain = jnp.maximum(equivalent - strength, 0.0) * stiff_inv
    factor = gain / jnp.maximum(equivalent, strength)
    keep = two_mu * (1.0 - three_mu * factor)
    pressure = bulk * trace
    stress = [pressure + keep * shape[c] for c in range(3)] + [keep * shape[c] for c in range(3, 6)]
    return stress, shape, (1.5 * two_mu) * factor, gain


def solve_rows(pieces, strain, out, props, green, plane, buffers):
    stx, eps, work, cos_ref, sin_ref = buffers
    ranks, rows, _, thickness, _ = pieces.shape

    def bring(c, carry):
        for h in range(ranks):
            stx[c, h * thickness : (h + 1) * thickness] = jnp.swapaxes(pieces[h, :, c], 0, 1)
        return carry

    lax.fori_loop(0, 7, bring, 0)
    for c in range(6):
        eps[c] = jnp.broadcast_to(strain[:, c : c + 1][None], (VOX_SIDE, rows, VOX_PLANE))

    def sweep(step, carry):
        for h in range(ranks):

            def law(place, inner, h=h):
                x = h * thickness + place
                strain = [eps[c, x] for c in range(6)]
                state = [stx[c, x] for c in range(7)]
                stress = voxel_law(strain, state, props.at[h], pl.ds(place, 1))[0]
                for c in range(6):
                    work[c, x] = stress[c]
                return inner

            lax.fori_loop(0, thickness, law, 0)

        def forward(c, inner):
            field = [work[c, x] for x in range(VOX_SIDE)]
            sums = [field[0]] + [field[x] + field[VOX_SIDE - x] for x in range(1, HALF)] + [field[HALF]]
            diffs = [None] + [field[x] - field[VOX_SIDE - x] for x in range(1, HALF)]
            for k, value in enumerate(cosine_line(sums)):
                cos_ref[c, k] = value
            for k, value in enumerate(sine_line(diffs)):
                if k > 0:
                    sin_ref[c, k - 1] = value
            return inner

        lax.fori_loop(0, 6, forward, 0)

        def transform():
            for ref, first in ((cos_ref, 0), (sin_ref, 2)):
                flat = ref[...].reshape(6 * ref.shape[1] * rows, VOX_PLANE)
                ref[...] = split_dot(flat, plane, first).reshape(ref.shape)

        def apply(field, k):
            row = pl.ds(k, 1)
            field = field[:3] + [2.0 * field[c] for c in range(3, 6)]
            total = [None] * 6
            for n, (i, j) in enumerate(PAIRS):
                entry = green[n, row, :]
                for a, b in [(i, j), (j, i)][: 1 + (i != j)]:
                    term = entry * field[b]
                    total[a] = term if total[a] is None else total[a] + term
            return total

        transform()
        for k in (0, HALF):
            result = apply([cos_ref[c, k] for c in range(6)], k)
            for c in range(6):
                cos_ref[c, k] = result[c]

        def mix(k, inner):
            even = [cos_ref[c, k] for c in range(6)]
            odd = [sin_ref[c, k - 1] for c in range(6)]
            ahead = apply([even[c] + odd[c] for c in range(6)], k)
            behind = apply([even[c] - odd[c] for c in range(6)], VOX_SIDE - k)
            for c in range(6):
                cos_ref[c, k] = ahead[c] + behind[c]
                sin_ref[c, k - 1] = ahead[c] - behind[c]
            return inner

        lax.fori_loop(1, HALF, mix, 0)
        transform()

        def backward(c, inner):
            even = cosine_line([cos_ref[c, k] for k in range(HALF + 1)])
            odd = sine_line([None] + [sin_ref[c, k - 1] for k in range(1, HALF)])
            eps[c, 0] = eps[c, 0] - even[0]
            eps[c, HALF] = eps[c, HALF] - even[HALF]
            for x in range(1, HALF):
                eps[c, x] = eps[c, x] - (even[x] + odd[x])
                eps[c, VOX_SIDE - x] = eps[c, VOX_SIDE - x] - (even[x] - odd[x])
            return inner

        lax.fori_loop(0, 6, backward, 0)
        return carry

    lax.fori_loop(0, SWEEPS, sweep, 0)
    totals = (jnp.zeros((rows, VOX_PLANE), jnp.float32),) * 6
    for h in range(ranks):

        def finish(place, totals, h=h):
            x = h * thickness + place
            strain = [eps[c, x] for c in range(6)]
            state = [stx[c, x] for c in range(7)]
            stress, shape, scale, gain = voxel_law(strain, state, props.at[h], pl.ds(place, 1))
            for c in range(6):
                stx[c, x] = state[c] + scale * shape[c]
            stx[6, x] = state[6] + gain
            return tuple(totals[c] + stress[c] for c in range(6))

        totals = lax.fori_loop(0, thickness, finish, totals)

    def give(c, carry):
        for h in range(ranks):
            out[h, :, c] = jnp.swapaxes(stx[c, h * thickness : (h + 1) * thickness], 0, 1)
        return carry

    lax.fori_loop(0, 7, give, 0)
    lane = lax.broadcasted_iota(jnp.int32, (rows, LANES), 1)
    means = jnp.zeros((rows, LANES), jnp.float32)
    for c in range(6):
        total = jnp.sum(totals[c], axis=1, keepdims=True) / VOX_SIDE**3
        means = jnp.where(lane == c, total, means)
    return means


def drain(ref, sem):
    pltpu.make_async_copy(ref, ref, sem).wait()


def exchange_kernel(
    raws,
    source_ref,
    note_ref,
    strain_ref,
    state_hbm,
    props_hbm,
    green_hbm,
    plane_hbm,
    got,
    mean_src_out,
    mean_raw_out,
    note_out,
    *scratch,
):
    (st, raw_send, raw_recv, ex_send, ex_recv, new_src, new_raw, props, green, plane) = scratch[:10]
    buffers = scratch[10:15]
    (note_recv, mean_src, mean_raw, mean_stage, load_sem, recv, sent) = scratch[15:]
    levels, groups = got.shape[:2]
    ranks, rows = ex_recv.shape[1:3]
    sources = levels - raws
    me, mine = lax.axis_index("macro"), lax.axis_index("vox")
    my_row, my_side = me // ranks, me % ranks
    R_PROPS, R_NOTE, R_RAW, R_MRAW, R_EX = 0, 1, 2, 3, 4
    R_MEAN, R_GOT = R_EX + sources, R_EX + 2 * sources

    def push(src, dst, kind, group, rank):
        pltpu.make_async_remote_copy(
            src_ref=src,
            dst_ref=dst,
            send_sem=sent.at[kind],
            recv_sem=recv.at[kind],
            device_id={"macro": group, "vox": rank},
            device_id_type=pl.DeviceIdType.MESH,
        ).start()

    def deliver(src, dst, kind, group, rank):
        here = (group == me) & (rank == mine)

        @pl.when(here)
        def _():
            pltpu.make_async_copy(src, dst, recv.at[kind]).start()

        @pl.when(jnp.logical_not(here))
        def _():
            push(src, dst, kind, group, rank)

    def settle(first, one_less, kind, fewer):
        @pl.when(fewer)
        def _():
            drain(one_less, sent.at[kind])

        @pl.when(jnp.logical_not(fewer))
        def _():
            drain(first, sent.at[kind])

    def turn(step, count, block, spot):
        planes = count // block
        line, lane = spot // block, spot % block
        ring = step // block
        line = jnp.where(2 * line < planes, planes - 1 - ring, ring)
        return line * block + (lane + step) % block

    state_copy = pltpu.make_async_copy(state_hbm, st, load_sem.at[0])
    state_copy.start()
    green_copy = pltpu.make_async_copy(green_hbm, green, load_sem.at[1])
    plane_copy = pltpu.make_async_copy(plane_hbm, plane, load_sem.at[2])
    props_copy = pltpu.make_async_copy(props_hbm, props.at[mine], load_sem.at[3])
    green_copy.start()
    plane_copy.start()
    props_copy.start()

    barrier = pltpu.get_barrier_semaphore()
    total = groups * ranks
    flat = me * ranks + mine

    def greet(k, carry):
        other = (flat + k) % total
        pl.semaphore_signal(
            barrier,
            inc=1,
            device_id={"macro": other // ranks, "vox": other % ranks},
            device_id_type=pl.DeviceIdType.MESH,
        )
        return carry

    lax.fori_loop(1, total, greet, 0)
    state_copy.wait()
    for lv in range(sources):
        for o in range(ranks):

            def gather(i, carry, lv=lv, o=o):
                slab = st[:, source_ref[lv * groups + ranks * i + (mine + o) % ranks]]
                if o == 0:
                    ex_recv[lv, mine, i] = slab
                else:
                    ex_send[lv, o - 1, i] = slab
                return carry

            lax.fori_loop(0, rows, gather, 0)
    if raws:

        def gather_raw(d, carry):
            raw_send[d] = st[:, source_ref[sources * groups + d]]
            return carry

        lax.fori_loop(0, groups, gather_raw, 0)
    pl.semaphore_wait(barrier, total - 1)

    for o in range(1, ranks):
        push(props_hbm, props.at[mine], R_PROPS, me, (mine + o) % ranks)

    def trade(lv):
        for o in range(1, ranks):
            push(ex_send.at[lv, o - 1], ex_recv.at[lv, mine], R_EX + lv, me, (mine + o) % ranks)

    trade(0)
    block = math.gcd(groups, 4)

    def send_note(t, carry):
        d = turn(t, groups, block, me)
        deliver(note_ref.at[d], note_recv.at[my_side * rows + my_row], R_NOTE, d, mine)
        return carry

    lax.fori_loop(0, groups, send_note, 0)
    if raws:

        def send_raw(t, carry):
            d = turn(t, groups, block, me)
            deliver(raw_send.at[d], raw_recv.at[mine, my_row], R_RAW, d, my_side)
            return carry

        lax.fori_loop(0, groups, send_raw, 0)
    for lv in range(1, sources):
        trade(lv)
    green_copy.wait()
    plane_copy.wait()
    props_copy.wait()
    if ranks > 1:
        drain(props.at[pl.ds(0, ranks - 1)], recv.at[R_PROPS])
    row_block = math.gcd(rows, 2)
    for lv in range(sources):
        if ranks > 1:
            drain(ex_recv.at[lv, pl.ds(0, ranks - 1)], recv.at[R_EX + lv])
        means = solve_rows(ex_recv.at[lv], strain_ref[lv], new_src.at[lv], props, green, plane, buffers)
        mean_src[lv, mine] = means
        for o in range(1, ranks):
            push(mean_src.at[lv, mine], mean_src.at[lv, mine], R_MEAN + lv, me, (mine + o) % ranks)

        def send_new(t, carry, lv=lv):
            i = turn(t, rows, row_block, my_row)
            for o in range(ranks):
                h = (mine + o) % ranks
                deliver(new_src.at[lv, h, i], got.at[lv, me], R_GOT + lv, ranks * i + mine, h)
            return carry

        lax.fori_loop(0, rows, send_new, 0)
    drain(note_recv, recv.at[R_NOTE])
    if raws:
        drain(raw_recv, recv.at[R_RAW])
        strain = note_recv[pl.ds(mine * rows, rows), 0, :]
        means = solve_rows(raw_recv, strain, new_raw, props, green, plane, buffers)
        for i in range(rows):
            mean_stage[i] = jnp.broadcast_to(means[i : i + 1, :], (8, LANES))

        def send_back(t, carry):
            i = turn(t, rows, row_block, my_row)
            for h in range(ranks):
                deliver(mean_stage.at[i], mean_raw.at[me], R_MRAW, ranks * i + mine, h)
            return carry

        lax.fori_loop(0, rows, send_back, 0)

        def send_done(i, carry):
            for o in range(ranks):
                h = (mine + o) % ranks
                deliver(new_raw.at[h, i], got.at[sources, ranks * i + mine], R_GOT + sources, me, h)
            return carry

        lax.fori_loop(0, rows, send_done, 0)
        drain(mean_raw, recv.at[R_MRAW])
    for lv in range(sources):
        if ranks > 1:
            drain(mean_src.at[lv, pl.ds(0, ranks - 1)], recv.at[R_MEAN + lv])
    mean_src_out[...] = mean_src[...]
    mean_raw_out[...] = mean_raw[:, 0, :]
    note_out[...] = note_recv[:, 0, :]
    for lv in range(levels):
        drain(got.at[lv], recv.at[R_GOT + lv])
    own = my_side == mine
    drain(note_ref.at[pl.ds(0, groups - 1)], sent.at[R_NOTE])
    if ranks > 1:
        drain(props.at[pl.ds(0, ranks - 1)], sent.at[R_PROPS])
    for lv in range(sources):
        if ranks > 1:
            drain(ex_send.at[lv], sent.at[R_EX + lv])
            drain(mean_src.at[lv, pl.ds(0, ranks - 1)], sent.at[R_MEAN + lv])
        settle(got.at[lv, pl.ds(0, groups)], got.at[lv, pl.ds(0, groups - 1)], R_GOT + lv, own)
    if raws:
        settle(raw_send, raw_send.at[pl.ds(0, groups - 1)], R_RAW, own)
        settle(mean_raw, mean_raw.at[pl.ds(0, groups - 1)], R_MRAW, own)
        if ranks > 1:
            drain(got.at[sources, pl.ds(0, groups - rows)], sent.at[R_GOT + sources])


def exchange(source, notes, strains, state, moduli, tables, raws):
    groups, ranks = lax.axis_size("macro"), lax.axis_size("vox")
    rows = groups // ranks
    thickness = state.shape[2]
    sources = strains.shape[0]
    levels = sources + raws
    slab = (7, thickness, VOX_PLANE)
    vmem = pl.BlockSpec(memory_space=pltpu.VMEM)
    anywhere = pl.BlockSpec(memory_space=pl.ANY)
    f32 = jnp.float32
    kinds = 4 + 2 * sources + levels
    cells = levels * VOX_SIDE * rows * VOX_PLANE
    return pl.pallas_call(
        functools.partial(exchange_kernel, raws),
        out_shape=[
            jax.ShapeDtypeStruct((levels, groups) + slab, f32),
            jax.ShapeDtypeStruct((sources, ranks, rows, LANES), f32),
            jax.ShapeDtypeStruct((groups, LANES), f32),
            jax.ShapeDtypeStruct((groups, LANES), f32),
        ],
        in_specs=[pl.BlockSpec(memory_space=pltpu.SMEM), vmem, vmem] + [anywhere] * 4,
        out_specs=[anywhere, vmem, vmem, vmem],
        scratch_shapes=[
            pltpu.VMEM(state.shape, f32),
            pltpu.VMEM((groups,) + slab, f32),
            pltpu.VMEM((ranks, rows) + slab, f32),
            pltpu.VMEM((sources, max(ranks - 1, 1), rows) + slab, f32),
            pltpu.VMEM((sources, ranks, rows) + slab, f32),
            pltpu.VMEM((sources, ranks, rows) + slab, f32),
            pltpu.VMEM((ranks, rows) + slab, f32),
            pltpu.VMEM((ranks,) + moduli.shape, f32),
            pltpu.VMEM(tables[0].shape, f32),
            pltpu.VMEM(tables[1].shape, tables[1].dtype),
            pltpu.VMEM((7, VOX_SIDE, rows, VOX_PLANE), f32),
            pltpu.VMEM((6, VOX_SIDE, rows, VOX_PLANE), f32),
            pltpu.VMEM((6, VOX_SIDE, rows, VOX_PLANE), f32),
            pltpu.VMEM((6, HALF + 1, rows, VOX_PLANE), f32),
            pltpu.VMEM((6, HALF - 1, rows, VOX_PLANE), f32),
            pltpu.VMEM((groups, 8, LANES), f32),
            pltpu.VMEM((sources, ranks, rows, LANES), f32),
            pltpu.VMEM((groups, 8, LANES), f32),
            pltpu.VMEM((rows, 8, LANES), f32),
            pltpu.SemaphoreType.DMA((4,)),
            pltpu.SemaphoreType.DMA((kinds,)),
            pltpu.SemaphoreType.DMA((kinds,)),
        ],
        compiler_params=pltpu.CompilerParams(
            collective_id=0, has_side_effects=True, vmem_limit_bytes=48 * 2**20
        ),
        cost_estimate=pl.CostEstimate(
            flops=SWEEPS * 2 * 3 * 2 * 6 * cells * VOX_PLANE,
            bytes_accessed=4 * 7 * cells * 4,
            transcendentals=SWEEPS * cells,
        ),
    )(source, notes, strains, state, moduli, *tables)


def pick_kernel(order_ref, got, out, sem):
    count = out.shape[1]
    groups = got.shape[1]

    def place(j, carry):
        slot = order_ref[j]
        pltpu.make_async_copy(got.at[slot // groups, slot % groups], out.at[:, j], sem).start()
        return carry

    lax.fori_loop(0, count, place, 0)
    drain(out, sem)


def pick_rows(order, got):
    shape = (7, order.shape[0]) + got.shape[3:]
    return pl.pallas_call(
        pick_kernel,
        out_shape=jax.ShapeDtypeStruct(shape, jnp.float32),
        in_specs=[pl.BlockSpec(memory_space=pltpu.SMEM), pl.BlockSpec(memory_space=pl.ANY)],
        out_specs=pl.BlockSpec(memory_space=pltpu.VMEM),
        scratch_shapes=[pltpu.SemaphoreType.DMA],
        compiler_params=pltpu.CompilerParams(vmem_limit_bytes=16 * 2**20),
    )(order, got)


def strain_tensor(disp_el, grad_el):
    products = [[jnp.sum(disp_el[i] * grad_el[j], axis=0) for j in range(3)] for i in range(3)]
    return jnp.stack(
        [
            products[0][0],
            products[1][1],
            products[2][2],
            0.5 * (products[1][2] + products[2][1]),
            0.5 * (products[0][2] + products[2][0]),
            0.5 * (products[0][1] + products[1][0]),
        ]
    )


def full_tensor(voigt):
    return [
        [voigt[0], voigt[5], voigt[4]],
        [voigt[5], voigt[1], voigt[3]],
        [voigt[4], voigt[3], voigt[2]],
    ]


def nodal_forces(stress, grad_el, volume):
    tensor = full_tensor(stress)
    return jnp.stack(
        [
            volume
            * (tensor[i][0] * grad_el[0] + tensor[i][1] * grad_el[1] + tensor[i][2] * grad_el[2])
            for i in range(3)
        ]
    )


def elastic_stress(strain, moduli):
    lame_first = moduli[0]
    shear_mod = moduli[1]
    trace = strain[0] + strain[1] + strain[2]
    return jnp.stack(
        [lame_first * trace + 2.0 * shear_mod * strain[c] for c in range(3)]
        + [2.0 * shear_mod * strain[c] for c in range(3, 6)]
    )


def local(
    displacement,
    load,
    conn,
    halo_list,
    grad_ops,
    volume,
    elastic_moduli,
    plastic_mask,
    new_owner,
    state,
    micro_moduli,
):
    groups = lax.axis_size("macro")
    ranks = lax.axis_size("vox")
    me = lax.axis_index("vox")
    own_nodes = displacement.shape[1]
    elements = conn.shape[1]
    rows = groups // ranks
    tables = (jnp.asarray(green_tables()), plane_tables())
    capacity = (PLASTIC_MAX + groups - 1) // groups
    raws = 1 if capacity > 1 else 0
    sources = capacity - raws
    plastic = plastic_mask == 1
    point_ids = jnp.arange(elements, dtype=jnp.int32)
    same_owner = (
        (new_owner[:, None] == new_owner[None, :])
        & plastic[:, None]
        & plastic[None, :]
        & (point_ids[None, :] < point_ids[:, None])
    )
    owner_rank = jnp.sum(same_owner.astype(jnp.int32), axis=1)
    send_slot = jnp.where(plastic, owner_rank * groups + new_owner, -1)
    slot_ids = jnp.arange(groups * capacity, dtype=jnp.int32)
    slot_match = slot_ids[:, None] == send_slot[None, :]
    match_float = slot_match.astype(jnp.float32)
    slot_source = jnp.sum(jnp.where(slot_match, point_ids[None, :], 0), axis=1)
    node_ids = jnp.arange(own_nodes, dtype=jnp.int32)
    halo_match = (halo_list[:, None] == node_ids[None, :]).astype(jnp.float32)
    halo_out = jnp.dot(displacement, halo_match.T, precision=FULL_PREC)
    halo_disp = shifted(halo_out, "macro", 1)
    local_disp = jnp.concatenate([displacement, halo_disp], axis=1)
    all_ids = jnp.arange(local_disp.shape[1], dtype=jnp.int32)
    node_match = (conn[:, :, None] == all_ids[None, None, :]).astype(jnp.float32)
    disp_el = jnp.einsum("in,aen->iae", local_disp, node_match, precision=FULL_PREC)
    strain = strain_tensor(disp_el, grad_ops)
    slot_strain = jnp.dot(match_float, strain.T, precision=FULL_PREC).reshape(capacity, groups, 6)
    valid = jnp.sum(match_float, axis=1).reshape(capacity, groups)
    note = jnp.concatenate(
        [slot_strain[capacity - 1], jnp.zeros((groups, 2), jnp.float32), valid.T], axis=1
    )
    note = jnp.pad(note, ((0, 0), (0, LANES - note.shape[1])))
    notes = jnp.broadcast_to(note[:, None, :], (groups, 8, LANES))
    own = slot_strain[:sources].reshape(sources, rows, ranks, 6)
    own = lax.dynamic_index_in_dim(own, me, 2, keepdims=False)
    strains = jnp.pad(own, ((0, 0), (0, 0), (0, LANES - 6)))
    got, mean_src, mean_raw, note_got = exchange(slot_source, notes, strains, state, micro_moduli, tables, raws)
    full = note_got[:, 8 : 8 + capacity].reshape(ranks, rows, capacity)
    full = jnp.swapaxes(full, 0, 1).reshape(-1) > 0.5
    places = slot_ids % capacity * groups + slot_ids // capacity
    earlier = (slot_ids[:, None] < slot_ids[None, :]) & full[:, None]
    position = jnp.sum(earlier.astype(jnp.int32), axis=0)
    wanted = jnp.arange(RECV_AGG, dtype=jnp.int32)
    wanted_match = (wanted[:, None] == position[None, :]) & full[None, :]
    order = jnp.sum(jnp.where(wanted_match, places[None, :], 0), axis=1)
    means = jnp.swapaxes(mean_src, 1, 2).reshape(sources * groups, LANES)
    if raws:
        means = jnp.concatenate([means, mean_raw], axis=0)
    stress_plastic = jnp.dot(means[:, :6].T, match_float, precision=FULL_PREC)
    stress = jnp.where(plastic[None, :], stress_plastic, elastic_stress(strain, elastic_moduli))
    forces = nodal_forces(stress, grad_ops, volume)
    assembled = jnp.einsum("iae,aen->in", forces, node_match, precision=FULL_PREC)
    returned_force = shifted(assembled[:, own_nodes:], "macro", -1)
    residual = (
        assembled[:, :own_nodes] + jnp.dot(returned_force, halo_match, precision=FULL_PREC) - load
    )
    return (residual, pick_rows(order, got))


def solution(mesh):
    return jax.shard_map(
        local,
        mesh=mesh,
        in_specs=(
            P(None, "macro"),
            P(None, "macro"),
            P(None, "macro"),
            P("macro"),
            P(None, None, "macro"),
            P("macro"),
            P(None, "macro"),
            P("macro"),
            P("macro"),
            P(None, "macro", "vox", None),
            P(None, "vox", None),
        ),
        out_specs=(P(None, "macro"), P(None, "macro", "vox", None)),
        check_vma=False,
    )
```

profile of v0, /device:TPU:0, one launch (start us, length us, event | category | flops | bytes accessed | tf_op | source)
XLA Modules:
  0.0 98.8 jit_solution(14417845517788541865)
XLA Ops:
  0.6 0.9 convolution_bitcast_fusion.1
  1.5 0.5 collective-permute-start
  2.0 0.7 broadcast_compare_fusion
  2.7 0.9 convert_reduce_fusion
  3.6 0.7 add_select_fusion
  4.3 0.1 select_reduce_fusion.source_ref
  4.4 0.1 convert_reduce_fusion.2
  4.5 0.1 reshape.223
  4.6 0.1 pad.16.clone
  4.7 3.5 %collective-permute-done = f32[3,16]{1,0:T(4,128)S(1)} collective-permute-done((f32[3,16]{1,0:T(4,128)S(1)}, f32[3,16]{1,0:T(4,128)S(1)}, u32[]{:S(2)}, u32[]{:S(2)}) %collective-permute-start) | collective-permute-done | bytes 224 | tf_op jit(solution)/shard_map/ppermute | solution.py:33
  8.2 1.2 %fusion.1 = f32[3,8,64]{2,0,1:T(4,128)S(1)} fusion(s32[8,64]{1,0:T(8,128)} %param.16, f32[3,16]{1,0:T(4,128)S(1)} %collective-permute-done, f32[3,64]{1,0:T(4,128)} %param.14), kind=kOutput, calls=%fused_computation.6 | convolution fusion | flops 1515760 | bytes 9152 | tf_op jit(solution)/shard_map/in,aen->iae/dot_general | solution.py:644
  9.4 0.8 multiply_reduce_fusion
  10.2 0.8 fusion.21
  11.0 0.7 multiply_add_fusion.1
  11.7 0.1 fusion.6
  11.8 0.1 slice.92
  11.9 0.1 pad_maximum_fusion.3
  12.0 0.1 copy.62
  12.0 0.1 copy.48
  12.2 0.7 copy-done
  13.0 1.0 %copy-done.1 = bf16[4,256,256]{2,1,0:T(8,128)(2,1)S(1)} copy-done((bf16[4,256,256]{2,1,0:T(8,128)(2,1)S(1)}, bf16[4,256,256]{2,1,0:T(8,128)(2,1)}, u32[]{:S(2)}) %copy-start.1) | copy-done | bytes 524312
  14.0 1.0 copy-done.2
  15.0 76.0 %shard_map.149 = (f32[3,16,7,8,256]{4,3,2,1,0:T(8,128)S(1)}, f32[2,2,8,128]{3,2,1,0:T(8,128)S(1)}, f32[16,128]{1,0:T(8,128)S(1)}, f32[16,128]{1,0:T(8,128)S(1)}) custom-call(s32[48]{0:T(128)S(1)} %select_reduce_fusion.source_ref, f32[16,8,128]{2,1,0:T(8,128)S(1)} %broadcast_in_dim.38.note_ref, f32[2,8,128]{2,1,0:T(8,128)S(1)} %pad.9.strain_ref, ...), custom_call_target="tpu_custom_call" | custom-call | flops 7247757312 | bytes 11010048 | tf_op jit(solution)/shard_map/pallas_call | solution.py:487
  91.1 0.2 convolution_select_fusion
  91.3 0.3 convolution_bitcast_fusion
  91.7 3.6 %collective-permute-start.1 = (f32[3,16]{1,0:T(4,128)S(1)}, f32[3,16]{1,0:T(4,128)S(1)}, u32[]{:S(2)}, u32[]{:S(2)}) collective-permute-start(f32[3,16]{1,0:T(4,128)S(1)} %slice.104), channel_id=1, source_target_pairs={{2,0},{4,2},{6,4},{8,6},{10,8},{12,10},{14,12},{16,14},{18,16},{20... | collective-permute-start | bytes 584 | tf_op jit(solution)/shard_map/ppermute | solution.py:33
  95.3 0.1 fusion.12
  95.4 0.1 gt.27
  95.5 0.1 convert_reduce_fusion.1
  95.6 0.1 select_reduce_fusion.1.order_ref
  95.7 2.3 %shard_map.150 = f32[7,24,8,256]{3,2,1,0:T(8,128)} custom-call(s32[24]{0:T(128)S(1)} %select_reduce_fusion.1.order_ref, f32[3,16,7,8,256]{4,3,2,1,0:T(8,128)S(1)} %get-tuple-element.9.got), custom_call_target="tpu_custom_call" | custom-call | tf_op jit(solution)/shard_map/pallas_call | solution.py:547
  98.0 0.8 fusion
  (29 shorter events, 0.3 us)
Async XLA Ops:
  1.5 6.7 %collective-permute-start = (f32[3,16]{1,0:T(4,128)S(1)}, f32[3,16]{1,0:T(4,128)S(1)}, u32[]{:S(2)}, u32[]{:S(2)}) collective-permute-start(f32[3,16]{1,0:T(4,128)S(1)} %convolution_bitcast_fusion.1), channel_id=1, source_target_pairs={{30,0},{0,2},{2,4},{4,6},{6,8},{8,10},{10,12},{12,14},{14,16},{16,... | collective-permute-start | bytes 584 | tf_op jit(solution)/shard_map/ppermute | solution.py:33
  12.2 0.8 copy-start
  13.0 1.0 %copy-start.1 = (bf16[4,256,256]{2,1,0:T(8,128)(2,1)S(1)}, bf16[4,256,256]{2,1,0:T(8,128)(2,1)}, u32[]{:S(2)}) copy-start(bf16[4,256,256]{2,1,0:T(8,128)(2,1)} %constant.69.plane_hbm) | copy-start | bytes 1572868
  14.0 1.0 copy-start.2
  15.0 76.3 %copy-start.3 = (f32[3,8,64]{2,1,0:T(8,128)S(1)}, f32[3,8,64]{2,1,0:T(8,128)}, u32[]{:S(2)}) copy-start(f32[3,8,64]{2,1,0:T(8,128)} %param.18) | copy-start | bytes 18436
  15.0 76.3 %copy-start.4 = (f32[64]{0:T(128)S(1)}, f32[64]{0:T(128)}, u32[]{:S(2)}) copy-start(f32[64]{0:T(128)} %param.19) | copy-start | bytes 772
  15.0 76.3 %copy-start.5 = (s32[8,64]{1,0:T(8,128)S(1)}, s32[8,64]{1,0:T(8,128)}, u32[]{:S(2)}) copy-start(s32[8,64]{1,0:T(8,128)} %param.16) | copy-start | bytes 6148
  91.0 7.0 %copy-start.6 = (f32[3,64]{1,0:T(4,128)S(1)}, f32[3,64]{1,0:T(4,128)}, u32[]{:S(2)}) copy-start(f32[3,64]{1,0:T(4,128)} %param.15) | copy-start | bytes 2308
  91.0 7.0 %copy-start.7 = (s32[16]{0:T(128)S(1)}, s32[16]{0:T(128)}, u32[]{:S(2)}) copy-start(s32[16]{0:T(128)} %param.17) | copy-start | bytes 196
  91.7 6.3 %collective-permute-start.1 = (f32[3,16]{1,0:T(4,128)S(1)}, f32[3,16]{1,0:T(4,128)S(1)}, u32[]{:S(2)}, u32[]{:S(2)}) collective-permute-start(f32[3,16]{1,0:T(4,128)S(1)} %slice.104), channel_id=1, source_target_pairs={{2,0},{4,2},{6,4},{8,6},{10,8},{12,10},{14,12},{16,14},{18,16},{20... | collective-permute-start | bytes 584 | tf_op jit(solution)/shard_map/ppermute | solution.py:33
where the time goes:
time: 99.3 us; the launch traced here: 98.8 us
  Pallas kernels  78.3 us (79%)
  other arithmetic  5.08 us (5%)
  starting transfers between devices  4.11 us (4%)
  local copies, waits for them, and re-layouts  3.55 us (4%)
  waiting for transfers between devices  3.55 us (4%)
  matrix products  3.41 us (3%)
    pallas_call x1, Pallas kernels, exchange(): pl.pallas_call(functools.partial(exchange_kernel, raws), out_shape=[jax.S...  76 us
    ppermute x2, starting transfers between devices, shifted(): return lax.ppermute(block, axis, route)  4.11 us
    ppermute x2, waiting for transfers between devices, shifted(): return lax.ppermute(block, axis, route)  3.55 us
    unnamed x17, local copies, waits for them, and re-layouts  2.89 us
    pallas_call x1, Pallas kernels, pick_rows(): pl.pallas_call(pick_kernel, out_shape=jax.ShapeDtypeStruct(shape, jnp.flo...  2.28 us
  transfers between devices with their start and end apart: 2, of which 1 were waited for; matrix products, arithmetic and copies ran while one was open for 3% of the time, Pallas kernels for 2%

commit v1 on v0

--- a/solution.py
+++ b/solution.py
@@ -19,18 +19,11 @@
 
 LAM_REF = 3.0
 MU_REF = 3.0
-FULL_PREC = lax.Precision.HIGHEST
 
 ROOT = math.sqrt(0.5)
 COS1 = math.cos(math.pi / 8)
 COS3 = math.cos(3 * math.pi / 8)
 PAIRS = [(i, j) for i in range(6) for j in range(i, 6)]
-
-
-def shifted(block, axis, distance):
-    devices = range(lax.axis_size(axis))
-    route = [((i - distance) % len(devices), i) for i in devices]
-    return lax.ppermute(block, axis, route)
 
 
 def green_tables():
@@ -267,31 +260,52 @@
     pltpu.make_async_copy(ref, ref, sem).wait()
 
 
-def exchange_kernel(
-    raws,
-    source_ref,
-    note_ref,
-    strain_ref,
-    state_hbm,
-    props_hbm,
-    green_hbm,
-    plane_hbm,
-    got,
-    mean_src_out,
-    mean_raw_out,
-    note_out,
-    *scratch,
-):
-    (st, raw_send, raw_recv, ex_send, ex_recv, new_src, new_raw, props, green, plane) = scratch[:10]
-    buffers = scratch[10:15]
-    (note_recv, mean_src, mean_raw, mean_stage, load_sem, recv, sent) = scratch[15:]
+def pieces_of(value):
+    high = value.astype(jnp.bfloat16)
+    rest = value - high.astype(jnp.float32)
+    middle = rest.astype(jnp.bfloat16)
+    low = (rest - middle.astype(jnp.float32)).astype(jnp.bfloat16)
+    return high, middle, low
+
+
+def select_dot(value, match, lanes):
+    contract = (((1,), (1 if lanes else 0,)), ((), ()))
+    parts = [
+        lax.dot_general(piece, match, contract, preferred_element_type=jnp.float32)
+        for piece in pieces_of(value)
+    ]
+    return parts[0] + (parts[1] + parts[2])
+
+
+def count_up(shape, axis):
+    return lax.broadcasted_iota(jnp.int32, shape, axis)
+
+
+def to_column(row, size):
+    spot = count_up((size, LANES), 0) == count_up((size, LANES), 1)
+    return jnp.sum(jnp.where(spot, row, 0.0), axis=1, keepdims=True)
+
+
+def exchange_kernel(raws, *refs):
+    (disp_hbm, load_hbm, conn_hbm, halo_hbm, grad_hbm, volume_hbm, moduli_hbm, owner_hbm) = refs[:8]
+    (state_hbm, props_hbm, green_hbm, plane_hbm) = refs[8:12]
+    got, residual, order_out = refs[12:15]
+    (st, raw_send, raw_recv, ex_send, ex_recv, new_src, new_raw, props, green, plane) = refs[15:25]
+    buffers = refs[25:30]
+    (note_send, note_recv, mean_src, mean_raw, mean_stage, mean_all) = refs[30:36]
+    (halo_send, halo_recv, force_send, force_recv, strain_ref, onehot, forces, rows_i) = refs[36:44]
+    (disp, load, conn, halo, grad, volume, moduli, owner, source_vec, source_ref) = refs[44:54]
+    load_sem, recv, sent = refs[54:]
     levels, groups = got.shape[:2]
     ranks, rows = ex_recv.shape[1:3]
+    own_nodes, elements, halos = disp.shape[1], conn.shape[1], halo.shape[1]
     sources = levels - raws
     me, mine = lax.axis_index("macro"), lax.axis_index("vox")
     my_row, my_side = me // ranks, me % ranks
-    R_PROPS, R_NOTE, R_RAW, R_MRAW, R_EX = 0, 1, 2, 3, 4
+    raw_side = (mine + ranks * groups - me) % ranks
+    R_PROPS, R_NOTE, R_RAW, R_MRAW, R_HALO, R_FORCE, R_EX = range(7)
     R_MEAN, R_GOT = R_EX + sources, R_EX + 2 * sources
+    f32 = jnp.float32
 
     def push(src, dst, kind, group, rank):
         pltpu.make_async_remote_copy(
@@ -314,14 +328,16 @@
         def _():
             push(src, dst, kind, group, rank)
 
-    def settle(first, one_less, kind, fewer):
+    def settle(ref, kind, fewer):
+        count = ref.shape[0]
+
         @pl.when(fewer)
         def _():
-            drain(one_less, sent.at[kind])
+            drain(ref.at[pl.ds(0, count - 1)], sent.at[kind])
 
         @pl.when(jnp.logical_not(fewer))
         def _():
-            drain(first, sent.at[kind])
+            drain(ref, sent.at[kind])
 
     def turn(step, count, block, spot):
         planes = count // block
@@ -330,14 +346,25 @@
         line = jnp.where(2 * line < planes, planes - 1 - ring, ring)
         return line * block + (lane + step) % block
 
-    state_copy = pltpu.make_async_copy(state_hbm, st, load_sem.at[0])
-    state_copy.start()
-    green_copy = pltpu.make_async_copy(green_hbm, green, load_sem.at[1])
-    plane_copy = pltpu.make_async_copy(plane_hbm, plane, load_sem.at[2])
-    props_copy = pltpu.make_async_copy(props_hbm, props.at[mine], load_sem.at[3])
-    green_copy.start()
-    plane_copy.start()
-    props_copy.start()
+    fetches = {}
+    for n, (src, dst) in enumerate(
+        (
+            (owner_hbm, owner),
+            (halo_hbm, halo),
+            (disp_hbm, disp),
+            (state_hbm, st),
+            (conn_hbm, conn),
+            (grad_hbm, grad),
+            (props_hbm, props.at[mine]),
+            (green_hbm, green),
+            (plane_hbm, plane),
+            (volume_hbm, volume),
+            (moduli_hbm, moduli),
+            (load_hbm, load),
+        )
+    ):
+        fetches[n] = pltpu.make_async_copy(src, dst, load_sem.at[n])
+        fetches[n].start()
 
     barrier = pltpu.get_barrier_semaphore()
     total = groups * ranks
@@ -354,12 +381,44 @@
         return carry
 
     lax.fori_loop(1, total, greet, 0)
-    state_copy.wait()
-    for lv in range(sources):
+
+    rows_i[...] = jnp.full(rows_i.shape, -1, jnp.int32)
+    fetches[0].wait()
+    rows_i[0:1, 0:elements] = owner[...]
+    owner_row = rows_i[0:1, :].astype(f32)
+    square = (LANES, LANES)
+    owner_col = to_column(owner_row, LANES)
+    before = count_up(square, 0) < count_up(square, 1)
+    same = (owner_col == owner_row) & before
+    rank_row = jnp.sum(jnp.where(same, 1.0, 0.0), axis=0, keepdims=True)
+    slot_row = jnp.where(owner_row >= 0.0, rank_row * groups + owner_row, -1.0)
+    slot_col = to_column(slot_row, LANES)
+    hit = slot_col == count_up(square, 1).astype(f32)
+    spots = jnp.where(hit, count_up(square, 0).astype(f32), 0.0)
+    source_vec[...] = jnp.sum(spots, axis=0, keepdims=True).astype(jnp.int32)
+    to_scalars = pltpu.make_async_copy(source_vec, source_ref, load_sem.at[12])
+    to_scalars.start()
+
+    fetches[1].wait()
+    fetches[2].wait()
+    rows_i[1:2, own_nodes : own_nodes + halos] = halo[...]
+    halo_match = (count_up(square, 0) == rows_i[1:2, :]).astype(jnp.bfloat16)
+    halo_send[...] = jnp.zeros(halo_send.shape, f32)
+    halo_send[0:3, 0:own_nodes] = disp[...]
+    own_disp = halo_send[...]
+    halo_send[...] = select_dot(own_disp, halo_match, False)
+
+    to_scalars.wait()
+    fetches[3].wait()
+
+    def slab_of(slot):
+        return st[:, jnp.clip(source_ref[0, slot], 0, elements - 1)]
+
+    def gather_trade(lv):
         for o in range(ranks):
 
-            def gather(i, carry, lv=lv, o=o):
-                slab = st[:, source_ref[lv * groups + ranks * i + (mine + o) % ranks]]
+            def gather(i, carry, o=o):
+                slab = slab_of(lv * groups + ranks * i + (mine + o) % ranks)
                 if o == 0:
                     ex_recv[lv, mine, i] = slab
                 else:
@@ -367,67 +426,159 @@
                 return carry
 
             lax.fori_loop(0, rows, gather, 0)
+
+    for lv in range(sources):
+        gather_trade(lv)
     if raws:
 
         def gather_raw(d, carry):
-            raw_send[d] = st[:, source_ref[sources * groups + d]]
+            raw_send[d] = slab_of(sources * groups + d)
             return carry
 
         lax.fori_loop(0, groups, gather_raw, 0)
     pl.semaphore_wait(barrier, total - 1)
 
-    for o in range(1, ranks):
-        push(props_hbm, props.at[mine], R_PROPS, me, (mine + o) % ranks)
+    row_block = math.gcd(rows, 2)
 
     def trade(lv):
         for o in range(1, ranks):
             push(ex_send.at[lv, o - 1], ex_recv.at[lv, mine], R_EX + lv, me, (mine + o) % ranks)
 
+    def send_raw(o):
+        side = (mine + o) % ranks
+
+        def step(t, carry):
+            d = ranks * turn(t, rows, row_block, my_row) + (side + ranks * groups - me) % ranks
+            deliver(raw_send.at[d], raw_recv.at[mine, my_row], R_RAW, d, side)
+            return carry
+
+        lax.fori_loop(0, rows, step, 0)
+
+    push(halo_send, halo_recv, R_HALO, (me + 1) % groups, mine)
+    for o in range(1, ranks):
+        push(props_hbm, props.at[mine], R_PROPS, me, (mine + o) % ranks)
     trade(0)
-    block = math.gcd(groups, 4)
+    if raws:
+        send_raw(0)
+
+    fetches[4].wait()
+    fetches[5].wait()
+    tall = (LANES, elements)
+    for a in range(conn.shape[0]):
+        onehot[a] = (count_up(tall, 0) == conn[a : a + 1, :]).astype(jnp.bfloat16)
+    drain(halo_recv, recv.at[R_HALO])
+    lane8 = count_up((8, LANES), 1)
+    near = jnp.where(lane8 < own_nodes, own_disp, halo_recv[...])
+    products = [jnp.zeros((8, elements), f32) for _ in range(3)]
+    for a in range(conn.shape[0]):
+        moved = select_dot(near, onehot[a], False)
+        for j in range(3):
+            products[j] = products[j] + moved * grad[j, a : a + 1, :]
+    strain_ref[...] = jnp.zeros(strain_ref.shape, f32)
+    strain_rows = [
+        products[0][0:1],
+        products[1][1:2],
+        products[2][2:3],
+        0.5 * (products[2][1:2] + products[1][2:3]),
+        0.5 * (products[2][0:1] + products[0][2:3]),
+        0.5 * (products[1][0:1] + products[0][1:2]),
+    ]
+    for c in range(6):
+        strain_ref[c : c + 1, 0:elements] = strain_rows[c]
+    all_strain = strain_ref[...]
+
+    def matched(ids):
+        return ids.astype(f32) == slot_row
+
+    wide = (groups, LANES)
+    note = jnp.zeros(wide, f32)
+    if raws:
+        hits = matched(count_up(wide, 0) + sources * groups)
+        match = jnp.where(hits, 1.0, 0.0).astype(jnp.bfloat16)
+        pieces = [
+            lax.dot_general(match, piece, (((1,), (1,)), ((), ())), preferred_element_type=f32)
+            for piece in pieces_of(all_strain)
+        ]
+        note = pieces[0] + (pieces[1] + pieces[2])
+    for lv in range(levels):
+        held = jnp.where(matched(count_up(wide, 0) + lv * groups), 1.0, 0.0)
+        note = jnp.where(count_up(wide, 1) == 8 + lv, jnp.sum(held, axis=1, keepdims=True), note)
+    for d in range(groups):
+        note_send[d] = jnp.broadcast_to(note[d : d + 1, :], (8, LANES))
 
     def send_note(t, carry):
-        d = turn(t, groups, block, me)
-        deliver(note_ref.at[d], note_recv.at[my_side * rows + my_row], R_NOTE, d, mine)
+        d = turn(t, groups, math.gcd(groups, 4), me)
+        deliver(note_send.at[d], note_recv.at[my_side * rows + my_row], R_NOTE, d, mine)
         return carry
 
     lax.fori_loop(0, groups, send_note, 0)
-    if raws:
-
-        def send_raw(t, carry):
-            d = turn(t, groups, block, me)
-            deliver(raw_send.at[d], raw_recv.at[mine, my_row], R_RAW, d, my_side)
-            return carry
-
-        lax.fori_loop(0, groups, send_raw, 0)
     for lv in range(1, sources):
         trade(lv)
-    green_copy.wait()
-    plane_copy.wait()
-    props_copy.wait()
+    if raws:
+        for o in range(1, ranks):
+            send_raw(o)
+    fetches[6].wait()
+    fetches[7].wait()
+    fetches[8].wait()
     if ranks > 1:
         drain(props.at[pl.ds(0, ranks - 1)], recv.at[R_PROPS])
-    row_block = math.gcd(rows, 2)
-    for lv in range(sources):
-        if ranks > 1:
-            drain(ex_recv.at[lv, pl.ds(0, ranks - 1)], recv.at[R_EX + lv])
-        means = solve_rows(ex_recv.at[lv], strain_ref[lv], new_src.at[lv], props, green, plane, buffers)
-        mean_src[lv, mine] = means
-        for o in range(1, ranks):
-            push(mean_src.at[lv, mine], mean_src.at[lv, mine], R_MEAN + lv, me, (mine + o) % ranks)
-
-        def send_new(t, carry, lv=lv):
+
+    def send_new(lv, low, high):
+        def step(t, carry):
             i = turn(t, rows, row_block, my_row)
             for o in range(ranks):
                 h = (mine + o) % ranks
                 deliver(new_src.at[lv, h, i], got.at[lv, me], R_GOT + lv, ranks * i + mine, h)
             return carry
 
-        lax.fori_loop(0, rows, send_new, 0)
+        lax.fori_loop(low, high, step, 0)
+
+    first, second = rows, rows
+    if raws:
+        first, second = rows // 4, rows - rows // 4
+    for lv in range(sources):
+        ids = lv * groups + ranks * count_up((rows, LANES), 0) + mine
+        match = jnp.where(matched(ids), 1.0, 0.0).astype(jnp.bfloat16)
+        pieces = [
+            lax.dot_general(match, piece, (((1,), (1,)), ((), ())), preferred_element_type=f32)
+            for piece in pieces_of(all_strain)
+        ]
+        strain = pieces[0] + (pieces[1] + pieces[2])
+        if ranks > 1:
+            drain(ex_recv.at[lv, pl.ds(0, ranks - 1)], recv.at[R_EX + lv])
+        means = solve_rows(ex_recv.at[lv], strain, new_src.at[lv], props, green, plane, buffers)
+        mean_src[lv, mine] = means
+        for o in range(1, ranks):
+            push(mean_src.at[lv, mine], mean_src.at[lv, mine], R_MEAN + lv, me, (mine + o) % ranks)
+        send_new(lv, 0, rows if lv < sources - 1 else first)
+
     drain(note_recv, recv.at[R_NOTE])
+    flags = note_recv[:, 0, :]
+    spot = count_up(wide, 0)
+    giver = (ranks * (spot % rows) + spot // rows).astype(f32)
+    lane = count_up(wide, 1)
+    counts = jnp.sum(jnp.where((lane >= 8) & (lane < 8 + levels), flags, 0.0), axis=1, keepdims=True)
+    tall_count = jnp.sum(
+        jnp.where(
+            (count_up(wide, 0) == lane) & (lane < groups), jnp.broadcast_to(counts, wide), 0.0
+        ),
+        axis=0,
+        keepdims=True,
+    )
+    lane_giver = (ranks * (lane % rows) + lane // rows).astype(f32)
+    earlier = (lane_giver < giver) & (lane < groups)
+    place = jnp.sum(jnp.where(earlier, tall_count, 0.0), axis=1, keepdims=True)
+    picks = jnp.zeros((1, LANES), f32)
+    for lv in range(levels):
+        held = jnp.sum(jnp.where(lane == 8 + lv, flags, 0.0), axis=1, keepdims=True)
+        chosen = (place == lane.astype(f32)) & (held > 0.5)
+        picks = picks + jnp.sum(jnp.where(chosen, lv * groups + giver, 0.0), axis=0, keepdims=True)
+        place = place + held
+    order_out[...] = picks.astype(jnp.int32)
+
     if raws:
         drain(raw_recv, recv.at[R_RAW])
-        strain = note_recv[pl.ds(mine * rows, rows), 0, :]
+        strain = note_recv[pl.ds(raw_side * rows, rows), 0, :]
         means = solve_rows(raw_recv, strain, new_raw, props, green, plane, buffers)
         for i in range(rows):
             mean_stage[i] = jnp.broadcast_to(means[i : i + 1, :], (8, LANES))
@@ -435,7 +586,7 @@
         def send_back(t, carry):
             i = turn(t, rows, row_block, my_row)
             for h in range(ranks):
-                deliver(mean_stage.at[i], mean_raw.at[me], R_MRAW, ranks * i + mine, h)
+                deliver(mean_stage.at[i], mean_raw.at[me], R_MRAW, ranks * i + raw_side, h)
             return carry
 
         lax.fori_loop(0, rows, send_back, 0)
@@ -443,57 +594,105 @@
         def send_done(i, carry):
             for o in range(ranks):
                 h = (mine + o) % ranks
-                deliver(new_raw.at[h, i], got.at[sources, ranks * i + mine], R_GOT + sources, me, h)
+                deliver(new_raw.at[h, i], got.at[sources, ranks * i + raw_side], R_GOT + sources, me, h)
             return carry
 
         lax.fori_loop(0, rows, send_done, 0)
-        drain(mean_raw, recv.at[R_MRAW])
+        send_new(sources - 1, first, second)
+
+    fetches[9].wait()
+    fetches[10].wait()
+    fetches[11].wait()
     for lv in range(sources):
         if ranks > 1:
             drain(mean_src.at[lv, pl.ds(0, ranks - 1)], recv.at[R_MEAN + lv])
-    mean_src_out[...] = mean_src[...]
-    mean_raw_out[...] = mean_raw[:, 0, :]
-    note_out[...] = note_recv[:, 0, :]
+        for y in range(ranks):
+            mean_all[lv * groups + y * rows : lv * groups + (y + 1) * rows, :] = mean_src[lv, y]
+    if raws:
+        drain(mean_raw, recv.at[R_MRAW])
+        mean_all[sources * groups :, :] = mean_raw[:, 0, :]
+    deep = (levels * groups, LANES)
+    k = count_up(deep, 0)
+    inside = k % groups
+    known = k - inside + jnp.where(
+        k < sources * groups, ranks * (inside % rows) + inside // rows, inside
+    )
+    match = jnp.where(matched(known), 1.0, 0.0).astype(jnp.bfloat16)
+    mean_t = jnp.transpose(mean_all[...])[0:8, :]
+    averaged = select_dot(mean_t, match, False)[:, 0:elements]
+    strain = all_strain[0:8, 0:elements]
+    lame, shear = moduli[0:1, :], moduli[1:2, :]
+    lateral = lame * (strain[0:1] + strain[1:2] + strain[2:3])
+    plastic = owner[...] >= 0
+    stress = []
+    for c in range(6):
+        plain = 2.0 * shear * strain[c : c + 1]
+        plain = lateral + plain if c < 3 else plain
+        stress.append(jnp.where(plastic, averaged[c : c + 1], plain))
+    tensor = [[stress[0], stress[5], stress[4]], [stress[5], stress[1], stress[3]], [stress[4], stress[3], stress[2]]]
+    forces[...] = jnp.zeros(forces.shape, f32)
+    for i in range(3):
+        force = volume[...] * (
+            tensor[i][0] * grad[0] + tensor[i][1] * grad[1] + tensor[i][2] * grad[2]
+        )
+        for a in range(conn.shape[0]):
+            forces[a, i : i + 1, :] = force[a : a + 1, :]
+    assembled = jnp.zeros((8, LANES), f32)
+    for a in range(conn.shape[0]):
+        assembled = assembled + select_dot(forces[a], onehot[a], True)
+    force_send[...] = assembled
+    push(force_send, force_recv, R_FORCE, (me + groups - 1) % groups, mine)
+    if raws:
+        send_new(sources - 1, second, rows)
+    drain(force_recv, recv.at[R_FORCE])
+    lane8 = count_up((8, LANES), 1)
+    beyond = (lane8 >= own_nodes) & (lane8 < own_nodes + halos)
+    back = jnp.where(beyond, force_recv[...], 0.0)
+    total_force = assembled + select_dot(back, halo_match, True)
+    residual[...] = total_force[0:3, 0:own_nodes] - load[...]
+
     for lv in range(levels):
         drain(got.at[lv], recv.at[R_GOT + lv])
-    own = my_side == mine
-    drain(note_ref.at[pl.ds(0, groups - 1)], sent.at[R_NOTE])
+    drain(note_send.at[pl.ds(0, groups - 1)], sent.at[R_NOTE])
+    drain(halo_send, sent.at[R_HALO])
+    drain(force_send, sent.at[R_FORCE])
     if ranks > 1:
         drain(props.at[pl.ds(0, ranks - 1)], sent.at[R_PROPS])
     for lv in range(sources):
         if ranks > 1:
             drain(ex_send.at[lv], sent.at[R_EX + lv])
             drain(mean_src.at[lv, pl.ds(0, ranks - 1)], sent.at[R_MEAN + lv])
-        settle(got.at[lv, pl.ds(0, groups)], got.at[lv, pl.ds(0, groups - 1)], R_GOT + lv, own)
+        settle(got.at[lv], R_GOT + lv, my_side == mine)
     if raws:
-        settle(raw_send, raw_send.at[pl.ds(0, groups - 1)], R_RAW, own)
-        settle(mean_raw, mean_raw.at[pl.ds(0, groups - 1)], R_MRAW, own)
+        own = (2 * me) % ranks == mine
+        settle(raw_send, R_RAW, own)
+        settle(mean_raw, R_MRAW, own)
         if ranks > 1:
             drain(got.at[sources, pl.ds(0, groups - rows)], sent.at[R_GOT + sources])
 
 
-def exchange(source, notes, strains, state, moduli, tables, raws):
+def exchange(smalls, state, moduli, tables, levels, raws):
     groups, ranks = lax.axis_size("macro"), lax.axis_size("vox")
     rows = groups // ranks
     thickness = state.shape[2]
-    sources = strains.shape[0]
-    levels = sources + raws
+    sources = levels - raws
+    nodes, corners, elements = smalls[0].shape[1], smalls[2].shape[0], smalls[2].shape[1]
     slab = (7, thickness, VOX_PLANE)
+    hbm = pl.BlockSpec(memory_space=pltpu.HBM)
     vmem = pl.BlockSpec(memory_space=pltpu.VMEM)
-    anywhere = pl.BlockSpec(memory_space=pl.ANY)
     f32 = jnp.float32
-    kinds = 4 + 2 * sources + levels
+    kinds = 7 + 2 * sources + levels
     cells = levels * VOX_SIDE * rows * VOX_PLANE
+    tile = pltpu.VMEM((8, LANES), f32)
     return pl.pallas_call(
         functools.partial(exchange_kernel, raws),
         out_shape=[
             jax.ShapeDtypeStruct((levels, groups) + slab, f32),
-            jax.ShapeDtypeStruct((sources, ranks, rows, LANES), f32),
-            jax.ShapeDtypeStruct((groups, LANES), f32),
-            jax.ShapeDtypeStruct((groups, LANES), f32),
+            jax.ShapeDtypeStruct((3, nodes), f32),
+            jax.ShapeDtypeStruct((1, LANES), jnp.int32),
         ],
-        in_specs=[pl.BlockSpec(memory_space=pltpu.SMEM), vmem, vmem] + [anywhere] * 4,
-        out_specs=[anywhere, vmem, vmem, vmem],
+        in_specs=[hbm] * (len(smalls) + 2 + len(tables)),
+        out_specs=[pl.BlockSpec(memory_space=pl.ANY), vmem, vmem],
         scratch_shapes=[
             pltpu.VMEM(state.shape, f32),
             pltpu.VMEM((groups,) + slab, f32),
@@ -511,10 +710,25 @@
             pltpu.VMEM((6, HALF + 1, rows, VOX_PLANE), f32),
             pltpu.VMEM((6, HALF - 1, rows, VOX_PLANE), f32),
             pltpu.VMEM((groups, 8, LANES), f32),
+            pltpu.VMEM((groups, 8, LANES), f32),
             pltpu.VMEM((sources, ranks, rows, LANES), f32),
             pltpu.VMEM((groups, 8, LANES), f32),
             pltpu.VMEM((rows, 8, LANES), f32),
-            pltpu.SemaphoreType.DMA((4,)),
+            pltpu.VMEM((levels * groups, LANES), f32),
+            tile,
+            tile,
+            tile,
+            tile,
+            pltpu.VMEM((LANES, LANES), f32),
+            pltpu.VMEM((corners, LANES, elements), jnp.bfloat16),
+            pltpu.VMEM((corners, 8, elements), f32),
+            pltpu.VMEM((8, LANES), jnp.int32),
+        ]
+        + [pltpu.VMEM(small.shape, small.dtype) for small in smalls]
+        + [
+            pltpu.VMEM((1, LANES), jnp.int32),
+            pltpu.SMEM((1, LANES), jnp.int32),
+            pltpu.SemaphoreType.DMA((13,)),
             pltpu.SemaphoreType.DMA((kinds,)),
             pltpu.SemaphoreType.DMA((kinds,)),
         ],
@@ -526,7 +740,7 @@
             bytes_accessed=4 * 7 * cells * 4,
             transcendentals=SWEEPS * cells,
         ),
-    )(source, notes, strains, state, moduli, *tables)
+    )(*smalls, state, moduli, *tables)
 
 
 def pick_kernel(order_ref, got, out, sem):
@@ -534,7 +748,7 @@
     groups = got.shape[1]
 
     def place(j, carry):
-        slot = order_ref[j]
+        slot = order_ref[0, j]
         pltpu.make_async_copy(got.at[slot // groups, slot % groups], out.at[:, j], sem).start()
         return carry
 
@@ -543,58 +757,14 @@
 
 
 def pick_rows(order, got):
-    shape = (7, order.shape[0]) + got.shape[3:]
     return pl.pallas_call(
         pick_kernel,
-        out_shape=jax.ShapeDtypeStruct(shape, jnp.float32),
+        out_shape=jax.ShapeDtypeStruct((7, RECV_AGG) + got.shape[3:], jnp.float32),
         in_specs=[pl.BlockSpec(memory_space=pltpu.SMEM), pl.BlockSpec(memory_space=pl.ANY)],
         out_specs=pl.BlockSpec(memory_space=pltpu.VMEM),
         scratch_shapes=[pltpu.SemaphoreType.DMA],
         compiler_params=pltpu.CompilerParams(vmem_limit_bytes=16 * 2**20),
     )(order, got)
-
-
-def strain_tensor(disp_el, grad_el):
-    products = [[jnp.sum(disp_el[i] * grad_el[j], axis=0) for j in range(3)] for i in range(3)]
-    return jnp.stack(
-        [
-            products[0][0],
-            products[1][1],
-            products[2][2],
-            0.5 * (products[1][2] + products[2][1]),
-            0.5 * (products[0][2] + products[2][0]),
-            0.5 * (products[0][1] + products[1][0]),
-        ]
-    )
-
-
-def full_tensor(voigt):
-    return [
-        [voigt[0], voigt[5], voigt[4]],
-        [voigt[5], voigt[1], voigt[3]],
-        [voigt[4], voigt[3], voigt[2]],
-    ]
-
-
-def nodal_forces(stress, grad_el, volume):
-    tensor = full_tensor(stress)
-    return jnp.stack(
-        [
-            volume
-            * (tensor[i][0] * grad_el[0] + tensor[i][1] * grad_el[1] + tensor[i][2] * grad_el[2])
-            for i in range(3)
-        ]
-    )
-
-
-def elastic_stress(strain, moduli):
-    lame_first = moduli[0]
-    shear_mod = moduli[1]
-    trace = strain[0] + strain[1] + strain[2]
-    return jnp.stack(
-        [lame_first * trace + 2.0 * shear_mod * strain[c] for c in range(3)]
-        + [2.0 * shear_mod * strain[c] for c in range(3, 6)]
-    )
 
 
 def local(
@@ -611,68 +781,20 @@
     micro_moduli,
 ):
     groups = lax.axis_size("macro")
-    ranks = lax.axis_size("vox")
-    me = lax.axis_index("vox")
-    own_nodes = displacement.shape[1]
-    elements = conn.shape[1]
-    rows = groups // ranks
     tables = (jnp.asarray(green_tables()), plane_tables())
-    capacity = (PLASTIC_MAX + groups - 1) // groups
-    raws = 1 if capacity > 1 else 0
-    sources = capacity - raws
-    plastic = plastic_mask == 1
-    point_ids = jnp.arange(elements, dtype=jnp.int32)
-    same_owner = (
-        (new_owner[:, None] == new_owner[None, :])
-        & plastic[:, None]
-        & plastic[None, :]
-        & (point_ids[None, :] < point_ids[:, None])
+    levels = (PLASTIC_MAX + groups - 1) // groups
+    raws = 1 if levels > 1 else 0
+    smalls = (
+        displacement,
+        load,
+        conn,
+        halo_list[None, :],
+        grad_ops,
+        volume[None, :],
+        elastic_moduli,
+        new_owner[None, :],
     )
-    owner_rank = jnp.sum(same_owner.astype(jnp.int32), axis=1)
-    send_slot = jnp.where(plastic, owner_rank * groups + new_owner, -1)
-    slot_ids = jnp.arange(groups * capacity, dtype=jnp.int32)
-    slot_match = slot_ids[:, None] == send_slot[None, :]
-    match_float = slot_match.astype(jnp.float32)
-    slot_source = jnp.sum(jnp.where(slot_match, point_ids[None, :], 0), axis=1)
-    node_ids = jnp.arange(own_nodes, dtype=jnp.int32)
-    halo_match = (halo_list[:, None] == node_ids[None, :]).astype(jnp.float32)
-    halo_out = jnp.dot(displacement, halo_match.T, precision=FULL_PREC)
-    halo_disp = shifted(halo_out, "macro", 1)
-    local_disp = jnp.concatenate([displacement, halo_disp], axis=1)
-    all_ids = jnp.arange(local_disp.shape[1], dtype=jnp.int32)
-    node_match = (conn[:, :, None] == all_ids[None, None, :]).astype(jnp.float32)
-    disp_el = jnp.einsum("in,aen->iae", local_disp, node_match, precision=FULL_PREC)
-    strain = strain_tensor(disp_el, grad_ops)
-    slot_strain = jnp.dot(match_float, strain.T, precision=FULL_PREC).reshape(capacity, groups, 6)
-    valid = jnp.sum(match_float, axis=1).reshape(capacity, groups)
-    note = jnp.concatenate(
-        [slot_strain[capacity - 1], jnp.zeros((groups, 2), jnp.float32), valid.T], axis=1
-    )
-    note = jnp.pad(note, ((0, 0), (0, LANES - note.shape[1])))
-    notes = jnp.broadcast_to(note[:, None, :], (groups, 8, LANES))
-    own = slot_strain[:sources].reshape(sources, rows, ranks, 6)
-    own = lax.dynamic_index_in_dim(own, me, 2, keepdims=False)
-    strains = jnp.pad(own, ((0, 0), (0, 0), (0, LANES - 6)))
-    got, mean_src, mean_raw, note_got = exchange(slot_source, notes, strains, state, micro_moduli, tables, raws)
-    full = note_got[:, 8 : 8 + capacity].reshape(ranks, rows, capacity)
-    full = jnp.swapaxes(full, 0, 1).reshape(-1) > 0.5
-    places = slot_ids % capacity * groups + slot_ids // capacity
-    earlier = (slot_ids[:, None] < slot_ids[None, :]) & full[:, None]
-    position = jnp.sum(earlier.astype(jnp.int32), axis=0)
-    wanted = jnp.arange(RECV_AGG, dtype=jnp.int32)
-    wanted_match = (wanted[:, None] == position[None, :]) & full[None, :]
-    order = jnp.sum(jnp.where(wanted_match, places[None, :], 0), axis=1)
-    means = jnp.swapaxes(mean_src, 1, 2).reshape(sources * groups, LANES)
-    if raws:
-        means = jnp.concatenate([means, mean_raw], axis=0)
-    stress_plastic = jnp.dot(means[:, :6].T, match_float, precision=FULL_PREC)
-    stress = jnp.where(plastic[None, :], stress_plastic, elastic_stress(strain, elastic_moduli))
-    forces = nodal_forces(stress, grad_ops, volume)
-    assembled = jnp.einsum("iae,aen->in", forces, node_match, precision=FULL_PREC)
-    returned_force = shifted(assembled[:, own_nodes:], "macro", -1)
-    residual = (
-        assembled[:, :own_nodes] + jnp.dot(returned_force, halo_match, precision=FULL_PREC) - load
-    )
+    got, residual, order = exchange(smalls, state, micro_moduli, tables, levels, raws)
     return (residual, pick_rows(order, got))
 
 

time: 99.3 us -> 94.7 us (0.954)
  Pallas kernels: 78.3 us -> 84.1 us
  local copies, waits for them, and re-layouts: 3.55 us -> 8.75 us
  other arithmetic: 5.08 us -> 0 us
  starting transfers between devices: 4.11 us -> 0 us
  waiting for transfers between devices: 3.55 us -> 0 us
  matrix products: 3.41 us -> 0 us
    unnamed x17 -> x23, local copies, waits for them, and re-layouts: 2.89 us -> 8.75 us
    pallas_call x1, Pallas kernels: 76 us -> 81.8 us  [exchange(): pl.pallas_call(functools.partial(exchange_kernel, raws), out_shape=[jax.S...]
    ppermute x2 -> x0, starting transfers between devices: 4.11 us -> none  [shifted(): return lax.ppermute(block, axis, route)]
    ppermute x2 -> x0, waiting for transfers between devices: 3.55 us -> none  [shifted(): return lax.ppermute(block, axis, route)]
    dot_general x6 -> x0, matrix products: 3.41 us -> none  [the longest x1 1.16 us: local(): jnp.einsum('in,aen->iae', local_disp, node_match, precision=FULL_PREC)]
    reduce_sum x6 -> x0, other arithmetic: 2.1 us -> none  [the longest x1 0.92 us: local(): owner_rank = jnp.sum(same_owner.astype(jnp.int32), axis=1)]
  transfers between devices with their start and end apart: 2 -> 0, of which waited for: 1 -> 0; matrix products, arithmetic and copies ran while one was open for 3% -> 0% of each run, Pallas kernels for 2% -> 0%
where the time goes in v1:
time: 94.7 us; the launch traced here: 93.5 us
  Pallas kernels  84.1 us (89%)
  local copies, waits for them, and re-layouts  8.75 us (9%)
    pallas_call x1, Pallas kernels, exchange(): pl.pallas_call(functools.partial(exchange_kernel, raws), out_shape=[jax.S...  81.8 us
    unnamed x23, local copies, waits for them, and re-layouts  8.75 us
    pallas_call x1, Pallas kernels, pick_rows(): pl.pallas_call(pick_kernel, out_shape=jax.ShapeDtypeStruct((7, RECV_AGG)...  2.27 us

profile of v1, /device:TPU:0, one launch (start us, length us, event | category | flops | bytes accessed | tf_op | source)
XLA Modules:
  0.0 93.5 jit_solution(18381174776333997935)
XLA Ops:
  0.6 0.0 copy-start
  0.6 0.7 copy-done
  1.4 0.0 copy-start.1
  1.4 0.7 copy-done.1
  2.1 0.0 copy-start.2
  2.1 0.7 copy-done.2
  2.8 0.0 copy-start.3
  2.8 0.7 copy-done.3
  3.5 0.0 copy-start.4
  3.5 0.7 copy-done.4
  4.2 0.0 copy-start.5
  4.2 0.7 copy-done.5
  4.8 0.0 copy-start.6
  4.8 0.7 copy-done.6
  5.5 0.0 copy-start.7
  5.5 0.7 copy-done.7
  6.1 0.0 copy-start.8
  6.1 0.7 copy-done.8
  6.8 0.0 copy-start.9
  6.8 1.0 %copy-done.9 = bf16[4,256,256]{2,1,0:T(8,128)(2,1)S(1)} copy-done((bf16[4,256,256]{2,1,0:T(8,128)(2,1)S(1)}, bf16[4,256,256]{2,1,0:T(8,128)(2,1)}, u32[]{:S(2)}) %copy-start.9) | copy-done | bytes 524312
  7.8 0.0 copy-start.10
  7.8 1.0 %copy-done.10 = f32[21,16,256]{2,1,0:T(8,128)S(1)} copy-done((f32[21,16,256]{2,1,0:T(8,128)S(1)}, f32[21,16,256]{2,1,0:T(8,128)}, u32[]{:S(2)}) %copy-start.10) | copy-done | bytes 344088
  8.8 81.8 %shard_map.140 = (f32[3,16,7,8,256]{4,3,2,1,0:T(8,128)S(1)}, f32[3,64]{1,0:T(4,128)S(1)}, s32[1,128]{1,0:T(1,128)S(1)}) custom-call(f32[3,64]{1,0:T(4,128)S(1)} %copy-done.3, f32[3,64]{1,0:T(4,128)S(1)} %copy-done.4, s32[8,64]{1,0:T(8,128)S(1)} %copy-done.2, s32[1,16]{1,0:T(1,128)S(1)} %bitcast.3, f32[3,8,64]{2,1,0:T(8,128)S(1)} %copy-done.1, ...), custom_call_target="tpu_custom_call" | custom-call | flops 7247757312 | bytes 11010048 | tf_op jit(solution)/shard_map/pallas_call | solution.py:687
  90.6 2.3 %shard_map.141 = f32[7,24,8,256]{3,2,1,0:T(8,128)} custom-call(s32[1,128]{1,0:T(1,128)S(1)} %get-tuple-element.6.order_ref, f32[3,16,7,8,256]{4,3,2,1,0:T(8,128)S(1)} %get-tuple-element.7.got), custom_call_target="tpu_custom_call" | custom-call | tf_op jit(solution)/shard_map/pallas_call | solution.py:760
  92.9 0.6 copy.16
Async XLA Ops:
  0.6 0.8 copy-start
  1.4 0.7 copy-start.1
  2.1 0.7 copy-start.2
  2.8 0.7 copy-start.3
  3.5 0.7 copy-start.4
  4.2 0.7 copy-start.5
  4.8 0.7 copy-start.6
  5.5 0.7 copy-start.7
  6.1 0.7 copy-start.8
  6.8 1.0 %copy-start.9 = (bf16[4,256,256]{2,1,0:T(8,128)(2,1)S(1)}, bf16[4,256,256]{2,1,0:T(8,128)(2,1)}, u32[]{:S(2)}) copy-start(bf16[4,256,256]{2,1,0:T(8,128)(2,1)} %constant.21.refs_11_) | copy-start | bytes 1572868
  7.8 1.0 %copy-start.10 = (f32[21,16,256]{2,1,0:T(8,128)S(1)}, f32[21,16,256]{2,1,0:T(8,128)}, u32[]{:S(2)}) copy-start(f32[21,16,256]{2,1,0:T(8,128)} %constant.6.clone.refs_10_) | copy-start | bytes 1032196

commit v2 on v1

--- a/solution.py
+++ b/solution.py
@@ -289,22 +289,23 @@
 def exchange_kernel(raws, *refs):
     (disp_hbm, load_hbm, conn_hbm, halo_hbm, grad_hbm, volume_hbm, moduli_hbm, owner_hbm) = refs[:8]
     (state_hbm, props_hbm, green_hbm, plane_hbm) = refs[8:12]
-    got, residual, order_out = refs[12:15]
-    (st, raw_send, raw_recv, ex_send, ex_recv, new_src, new_raw, props, green, plane) = refs[15:25]
-    buffers = refs[25:30]
-    (note_send, note_recv, mean_src, mean_raw, mean_stage, mean_all) = refs[30:36]
-    (halo_send, halo_recv, force_send, force_recv, strain_ref, onehot, forces, rows_i) = refs[36:44]
-    (disp, load, conn, halo, grad, volume, moduli, owner, source_vec, source_ref) = refs[44:54]
-    load_sem, recv, sent = refs[54:]
-    levels, groups = got.shape[:2]
-    ranks, rows = ex_recv.shape[1:3]
+    residual, moved_out = refs[12:14]
+    (st, raw_send, raw_recv, ex_send, ex_recv, new_src, new_raw, props, green, plane) = refs[14:24]
+    buffers = refs[24:29]
+    (note_send, note_recv, mean_src, mean_raw, mean_stage, mean_all) = refs[29:35]
+    (halo_send, halo_recv, force_send, force_recv, strain_ref, onehot, forces, rows_i) = refs[35:43]
+    (disp, load, conn, halo, grad, volume, moduli, owner) = refs[43:51]
+    (source_vec, source_ref, order_vec, order_ref, got, load_sem, recv, sent) = refs[51:]
+    sources, ranks, rows = ex_recv.shape[:3]
+    groups, levels = ranks * rows, sources + raws
     own_nodes, elements, halos = disp.shape[1], conn.shape[1], halo.shape[1]
-    sources = levels - raws
     me, mine = lax.axis_index("macro"), lax.axis_index("vox")
     my_row, my_side = me // ranks, me % ranks
     raw_side = (mine + ranks * groups - me) % ranks
-    R_PROPS, R_NOTE, R_RAW, R_MRAW, R_HALO, R_FORCE, R_EX = range(7)
+    R_PROPS, R_NOTE, R_HALO, R_FORCE, R_EX = range(5)
     R_MEAN, R_GOT = R_EX + sources, R_EX + 2 * sources
+    R_RAW = R_GOT + levels
+    R_MRAW = R_RAW + raws
     f32 = jnp.float32
 
     def push(src, dst, kind, group, rank):
@@ -429,10 +430,10 @@
 
     for lv in range(sources):
         gather_trade(lv)
-    if raws:
-
-        def gather_raw(d, carry):
-            raw_send[d] = slab_of(sources * groups + d)
+    for q in range(raws):
+
+        def gather_raw(d, carry, q=q):
+            raw_send[q, d] = slab_of((sources + q) * groups + d)
             return carry
 
         lax.fori_loop(0, groups, gather_raw, 0)
@@ -444,12 +445,12 @@
         for o in range(1, ranks):
             push(ex_send.at[lv, o - 1], ex_recv.at[lv, mine], R_EX + lv, me, (mine + o) % ranks)
 
-    def send_raw(o):
+    def send_raw(q, o):
         side = (mine + o) % ranks
 
         def step(t, carry):
             d = ranks * turn(t, rows, row_block, my_row) + (side + ranks * groups - me) % ranks
-            deliver(raw_send.at[d], raw_recv.at[mine, my_row], R_RAW, d, side)
+            deliver(raw_send.at[q, d], raw_recv.at[q, mine, my_row], R_RAW + q, d, side)
             return carry
 
         lax.fori_loop(0, rows, step, 0)
@@ -459,7 +460,7 @@
         push(props_hbm, props.at[mine], R_PROPS, me, (mine + o) % ranks)
     trade(0)
     if raws:
-        send_raw(0)
+        send_raw(0, 0)
 
     fetches[4].wait()
     fetches[5].wait()
@@ -492,14 +493,19 @@
 
     wide = (groups, LANES)
     note = jnp.zeros(wide, f32)
-    if raws:
-        hits = matched(count_up(wide, 0) + sources * groups)
-        match = jnp.where(hits, 1.0, 0.0).astype(jnp.bfloat16)
-        pieces = [
+    strain_pieces = pieces_of(all_strain)
+
+    def strain_of(ids):
+        match = jnp.where(matched(ids), 1.0, 0.0).astype(jnp.bfloat16)
+        parts = [
             lax.dot_general(match, piece, (((1,), (1,)), ((), ())), preferred_element_type=f32)
-            for piece in pieces_of(all_strain)
+            for piece in strain_pieces
         ]
-        note = pieces[0] + (pieces[1] + pieces[2])
+        return parts[0] + (parts[1] + parts[2])
+
+    for q in range(raws):
+        held = strain_of(count_up(wide, 0) + (sources + q) * groups)
+        note = note + (pltpu.roll(held, 16 * q, 1) if q else held)
     for lv in range(levels):
         held = jnp.where(matched(count_up(wide, 0) + lv * groups), 1.0, 0.0)
         note = jnp.where(count_up(wide, 1) == 8 + lv, jnp.sum(held, axis=1, keepdims=True), note)
@@ -512,45 +518,41 @@
         return carry
 
     lax.fori_loop(0, groups, send_note, 0)
-    for lv in range(1, sources):
-        trade(lv)
-    if raws:
-        for o in range(1, ranks):
-            send_raw(o)
     fetches[6].wait()
     fetches[7].wait()
     fetches[8].wait()
     if ranks > 1:
         drain(props.at[pl.ds(0, ranks - 1)], recv.at[R_PROPS])
 
-    def send_new(lv, low, high):
+    def send_new(lv, low, high, turns):
         def step(t, carry):
             i = turn(t, rows, row_block, my_row)
-            for o in range(ranks):
+            for o in turns:
                 h = (mine + o) % ranks
-                deliver(new_src.at[lv, h, i], got.at[lv, me], R_GOT + lv, ranks * i + mine, h)
+                deliver(new_src.at[lv, h, i], got.at[lv * groups + me], R_GOT + lv, ranks * i + mine, h)
             return carry
 
         lax.fori_loop(low, high, step, 0)
 
-    first, second = rows, rows
-    if raws:
-        first, second = rows // 4, rows - rows // 4
+    near, far = range(1), range(1, ranks)
+    early = rows // 2 if raws else rows
     for lv in range(sources):
         ids = lv * groups + ranks * count_up((rows, LANES), 0) + mine
-        match = jnp.where(matched(ids), 1.0, 0.0).astype(jnp.bfloat16)
-        pieces = [
-            lax.dot_general(match, piece, (((1,), (1,)), ((), ())), preferred_element_type=f32)
-            for piece in pieces_of(all_strain)
-        ]
-        strain = pieces[0] + (pieces[1] + pieces[2])
+        strain = strain_of(ids)
         if ranks > 1:
             drain(ex_recv.at[lv, pl.ds(0, ranks - 1)], recv.at[R_EX + lv])
+        if lv == 0:
+            for later in range(1, sources):
+                trade(later)
+            if raws:
+                for o in range(1, ranks):
+                    send_raw(0, o)
         means = solve_rows(ex_recv.at[lv], strain, new_src.at[lv], props, green, plane, buffers)
         mean_src[lv, mine] = means
         for o in range(1, ranks):
             push(mean_src.at[lv, mine], mean_src.at[lv, mine], R_MEAN + lv, me, (mine + o) % ranks)
-        send_new(lv, 0, rows if lv < sources - 1 else first)
+        if not raws:
+            send_new(lv, 0, rows, range(ranks))
 
     drain(note_recv, recv.at[R_NOTE])
     flags = note_recv[:, 0, :]
@@ -574,31 +576,42 @@
         chosen = (place == lane.astype(f32)) & (held > 0.5)
         picks = picks + jnp.sum(jnp.where(chosen, lv * groups + giver, 0.0), axis=0, keepdims=True)
         place = place + held
-    order_out[...] = picks.astype(jnp.int32)
-
-    if raws:
-        drain(raw_recv, recv.at[R_RAW])
-        strain = note_recv[pl.ds(raw_side * rows, rows), 0, :]
-        means = solve_rows(raw_recv, strain, new_raw, props, green, plane, buffers)
+    order_vec[...] = picks.astype(jnp.int32)
+    order_scalars = pltpu.make_async_copy(order_vec, order_ref, load_sem.at[12])
+    order_scalars.start()
+
+    for q in range(raws):
+        drain(raw_recv.at[q], recv.at[R_RAW + q])
+        if q + 1 < raws:
+            for o in range(ranks):
+                send_raw(q + 1, o)
+        else:
+            for lv in range(sources):
+                send_new(lv, 0, rows, far)
+                send_new(lv, 0, early, near)
+        strain = pltpu.roll(note_recv[pl.ds(raw_side * rows, rows), 0, :], LANES - 16 * q, 1)
+        means = solve_rows(raw_recv.at[q], strain, new_raw.at[q], props, green, plane, buffers)
         for i in range(rows):
-            mean_stage[i] = jnp.broadcast_to(means[i : i + 1, :], (8, LANES))
-
-        def send_back(t, carry):
+            mean_stage[q, i] = jnp.broadcast_to(means[i : i + 1, :], (8, LANES))
+
+        def send_back(t, carry, q=q):
             i = turn(t, rows, row_block, my_row)
             for h in range(ranks):
-                deliver(mean_stage.at[i], mean_raw.at[me], R_MRAW, ranks * i + raw_side, h)
+                deliver(mean_stage.at[q, i], mean_raw.at[q, me], R_MRAW + q, ranks * i + raw_side, h)
             return carry
 
         lax.fori_loop(0, rows, send_back, 0)
 
-        def send_done(i, carry):
+        def send_done(i, carry, q=q):
             for o in range(ranks):
                 h = (mine + o) % ranks
-                deliver(new_raw.at[h, i], got.at[sources, ranks * i + raw_side], R_GOT + sources, me, h)
+                spot = (sources + q) * groups + ranks * i + raw_side
+                deliver(new_raw.at[q, h, i], got.at[spot], R_GOT + sources + q, me, h)
             return carry
 
         lax.fori_loop(0, rows, send_done, 0)
-        send_new(sources - 1, first, second)
+    for lv in range(sources):
+        send_new(lv, early, rows, near)
 
     fetches[9].wait()
     fetches[10].wait()
@@ -608,9 +621,10 @@
             drain(mean_src.at[lv, pl.ds(0, ranks - 1)], recv.at[R_MEAN + lv])
         for y in range(ranks):
             mean_all[lv * groups + y * rows : lv * groups + (y + 1) * rows, :] = mean_src[lv, y]
-    if raws:
-        drain(mean_raw, recv.at[R_MRAW])
-        mean_all[sources * groups :, :] = mean_raw[:, 0, :]
+    for q in range(raws):
+        drain(mean_raw.at[q], recv.at[R_MRAW + q])
+        low = (sources + q) * groups
+        mean_all[low : low + groups, :] = mean_raw[q, :, 0, :]
     deep = (levels * groups, LANES)
     k = count_up(deep, 0)
     inside = k % groups
@@ -642,8 +656,6 @@
         assembled = assembled + select_dot(forces[a], onehot[a], True)
     force_send[...] = assembled
     push(force_send, force_recv, R_FORCE, (me + groups - 1) % groups, mine)
-    if raws:
-        send_new(sources - 1, second, rows)
     drain(force_recv, recv.at[R_FORCE])
     lane8 = count_up((8, LANES), 1)
     beyond = (lane8 >= own_nodes) & (lane8 < own_nodes + halos)
@@ -652,7 +664,14 @@
     residual[...] = total_force[0:3, 0:own_nodes] - load[...]
 
     for lv in range(levels):
-        drain(got.at[lv], recv.at[R_GOT + lv])
+        drain(got.at[pl.ds(lv * groups, groups)], recv.at[R_GOT + lv])
+    order_scalars.wait()
+
+    def place_row(j, carry):
+        moved_out[:, j] = got[jnp.clip(order_ref[0, j], 0, levels * groups - 1)]
+        return carry
+
+    lax.fori_loop(0, moved_out.shape[1], place_row, 0)
     drain(note_send.at[pl.ds(0, groups - 1)], sent.at[R_NOTE])
     drain(halo_send, sent.at[R_HALO])
     drain(force_send, sent.at[R_FORCE])
@@ -662,13 +681,13 @@
         if ranks > 1:
             drain(ex_send.at[lv], sent.at[R_EX + lv])
             drain(mean_src.at[lv, pl.ds(0, ranks - 1)], sent.at[R_MEAN + lv])
-        settle(got.at[lv], R_GOT + lv, my_side == mine)
-    if raws:
-        own = (2 * me) % ranks == mine
-        settle(raw_send, R_RAW, own)
-        settle(mean_raw, R_MRAW, own)
+        settle(got.at[pl.ds(0, groups)], R_GOT + lv, my_side == mine)
+    own = (2 * me) % ranks == mine
+    for q in range(raws):
+        settle(raw_send.at[q], R_RAW + q, own)
+        settle(mean_raw.at[q], R_MRAW + q, own)
         if ranks > 1:
-            drain(got.at[sources, pl.ds(0, groups - rows)], sent.at[R_GOT + sources])
+            drain(got.at[pl.ds(0, groups - rows)], sent.at[R_GOT + sources + q])
 
 
 def exchange(smalls, state, moduli, tables, levels, raws):
@@ -681,26 +700,25 @@
     hbm = pl.BlockSpec(memory_space=pltpu.HBM)
     vmem = pl.BlockSpec(memory_space=pltpu.VMEM)
     f32 = jnp.float32
-    kinds = 7 + 2 * sources + levels
+    kinds = 5 + 2 * sources + levels + 2 * raws
     cells = levels * VOX_SIDE * rows * VOX_PLANE
     tile = pltpu.VMEM((8, LANES), f32)
     return pl.pallas_call(
         functools.partial(exchange_kernel, raws),
         out_shape=[
-            jax.ShapeDtypeStruct((levels, groups) + slab, f32),
             jax.ShapeDtypeStruct((3, nodes), f32),
-            jax.ShapeDtypeStruct((1, LANES), jnp.int32),
+            jax.ShapeDtypeStruct((7, RECV_AGG) + slab[1:], f32),
         ],
         in_specs=[hbm] * (len(smalls) + 2 + len(tables)),
-        out_specs=[pl.BlockSpec(memory_space=pl.ANY), vmem, vmem],
+        out_specs=[vmem, vmem],
         scratch_shapes=[
             pltpu.VMEM(state.shape, f32),
-            pltpu.VMEM((groups,) + slab, f32),
-            pltpu.VMEM((ranks, rows) + slab, f32),
+            pltpu.VMEM((max(raws, 1), groups) + slab, f32),
+            pltpu.VMEM((max(raws, 1), ranks, rows) + slab, f32),
             pltpu.VMEM((sources, max(ranks - 1, 1), rows) + slab, f32),
             pltpu.VMEM((sources, ranks, rows) + slab, f32),
             pltpu.VMEM((sources, ranks, rows) + slab, f32),
-            pltpu.VMEM((ranks, rows) + slab, f32),
+            pltpu.VMEM((max(raws, 1), ranks, rows) + slab, f32),
             pltpu.VMEM((ranks,) + moduli.shape, f32),
             pltpu.VMEM(tables[0].shape, f32),
             pltpu.VMEM(tables[1].shape, tables[1].dtype),
@@ -712,8 +730,8 @@
             pltpu.VMEM((groups, 8, LANES), f32),
             pltpu.VMEM((groups, 8, LANES), f32),
             pltpu.VMEM((sources, ranks, rows, LANES), f32),
-            pltpu.VMEM((groups, 8, LANES), f32),
-            pltpu.VMEM((rows, 8, LANES), f32),
+            pltpu.VMEM((max(raws, 1), groups, 8, LANES), f32),
+            pltpu.VMEM((max(raws, 1), rows, 8, LANES), f32),
             pltpu.VMEM((levels * groups, LANES), f32),
             tile,
             tile,
@@ -728,12 +746,15 @@
         + [
             pltpu.VMEM((1, LANES), jnp.int32),
             pltpu.SMEM((1, LANES), jnp.int32),
+            pltpu.VMEM((1, LANES), jnp.int32),
+            pltpu.SMEM((1, LANES), jnp.int32),
+            pltpu.VMEM((levels * groups,) + slab, f32),
             pltpu.SemaphoreType.DMA((13,)),
             pltpu.SemaphoreType.DMA((kinds,)),
             pltpu.SemaphoreType.DMA((kinds,)),
         ],
         compiler_params=pltpu.CompilerParams(
-            collective_id=0, has_side_effects=True, vmem_limit_bytes=48 * 2**20
+            collective_id=0, has_side_effects=True, vmem_limit_bytes=63 * 2**20
         ),
         cost_estimate=pl.CostEstimate(
             flops=SWEEPS * 2 * 3 * 2 * 6 * cells * VOX_PLANE,
@@ -741,30 +762,6 @@
             transcendentals=SWEEPS * cells,
         ),
     )(*smalls, state, moduli, *tables)
-
-
-def pick_kernel(order_ref, got, out, sem):
-    count = out.shape[1]
-    groups = got.shape[1]
-
-    def place(j, carry):
-        slot = order_ref[0, j]
-        pltpu.make_async_copy(got.at[slot // groups, slot % groups], out.at[:, j], sem).start()
-        return carry
-
-    lax.fori_loop(0, count, place, 0)
-    drain(out, sem)
-
-
-def pick_rows(order, got):
-    return pl.pallas_call(
-        pick_kernel,
-        out_shape=jax.ShapeDtypeStruct((7, RECV_AGG) + got.shape[3:], jnp.float32),
-        in_specs=[pl.BlockSpec(memory_space=pltpu.SMEM), pl.BlockSpec(memory_space=pl.ANY)],
-        out_specs=pl.BlockSpec(memory_space=pltpu.VMEM),
-        scratch_shapes=[pltpu.SemaphoreType.DMA],
-        compiler_params=pltpu.CompilerParams(vmem_limit_bytes=16 * 2**20),
-    )(order, got)
 
 
 def local(
@@ -783,7 +780,7 @@
     groups = lax.axis_size("macro")
     tables = (jnp.asarray(green_tables()), plane_tables())
     levels = (PLASTIC_MAX + groups - 1) // groups
-    raws = 1 if levels > 1 else 0
+    raws = levels - 1
     smalls = (
         displacement,
         load,
@@ -794,8 +791,7 @@
         elastic_moduli,
         new_owner[None, :],
     )
-    got, residual, order = exchange(smalls, state, micro_moduli, tables, levels, raws)
-    return (residual, pick_rows(order, got))
+    return tuple(exchange(smalls, state, micro_moduli, tables, levels, raws))
 
 
 def solution(mesh):

time: 94.7 us -> 86.3 us (0.911)
  local copies, waits for them, and re-layouts: 8.75 us -> 3.79 us
  Pallas kernels: 84.1 us -> 81.2 us
    unnamed x23 -> x2, local copies, waits for them, and re-layouts: 8.75 us -> 3.79 us
    pallas_call x1 -> x0, Pallas kernels: 2.27 us -> none  [pick_rows(): pl.pallas_call(pick_kernel, out_shape=jax.ShapeDtypeStruct((7, RECV_AGG)...]
where the time goes in v2:
time: 86.3 us; the launch traced here: 85.7 us
  Pallas kernels  81.2 us (94%)
  local copies, waits for them, and re-layouts  3.79 us (4%)
    pallas_call x1, Pallas kernels, exchange(): pl.pallas_call(functools.partial(exchange_kernel, raws), out_shape=[jax.S...  81.2 us
    unnamed x2, local copies, waits for them, and re-layouts  3.79 us

profile of v2, /device:TPU:0, one launch (start us, length us, event | category | flops | bytes accessed | tf_op | source)
XLA Modules:
  0.0 85.7 jit_solution(7562424833696073385)
XLA Ops:
  0.6 81.2 %shard_map.140 = (f32[3,64]{1,0:T(4,128)}, f32[7,24,8,256]{3,2,1,0:T(8,128)}) custom-call(f32[3,64]{1,0:T(4,128)} %refs_0_.1, f32[3,64]{1,0:T(4,128)} %refs_1_.1, s32[8,64]{1,0:T(8,128)} %refs_2_.1, s32[1,16]{1,0:T(1,128)} %bitcast.3, f32[3,8,64]{2,1,0:T(8,128)} %refs_4_.1, f32[1,64]{1,0:T(1,128)} %bitcast.4, f32[2,64]{1,0:T(2,128)} %refs_6_.1, ...), custom_call_target="tpu_custom_call" | custom-call | flops 7247757312 | bytes 11010048 | tf_op jit(solution)/shard_map/pallas_call | solution.py:706
  81.9 1.2 %copy.17 = f32[3,64]{1,0:T(4,128)} copy(f32[3,64]{1,0:T(4,128)} %get-tuple-element.4) | data formatting | bytes 1536
  83.1 2.5 %copy.18 = f32[7,24,8,256]{3,2,1,0:T(8,128)} copy(f32[7,24,8,256]{3,2,1,0:T(8,128)} %get-tuple-element.5) | data formatting | bytes 2752512

commit v3 on v2

--- a/solution.py
+++ b/solution.py
@@ -138,7 +138,7 @@
     return stress, shape, (1.5 * two_mu) * factor, gain
 
 
-def solve_rows(pieces, strain, out, props, green, plane, buffers):
+def solve_rows(pieces, strain, base, out, props, green, plane, buffers):
     stx, eps, work, cos_ref, sin_ref = buffers
     ranks, rows, _, thickness, _ = pieces.shape
 
@@ -149,7 +149,7 @@
 
     lax.fori_loop(0, 7, bring, 0)
     for c in range(6):
-        eps[c] = jnp.broadcast_to(strain[:, c : c + 1][None], (VOX_SIDE, rows, VOX_PLANE))
+        eps[c] = jnp.broadcast_to(strain[:, base + c : base + c + 1][None], (VOX_SIDE, rows, VOX_PLANE))
 
     def sweep(step, carry):
         for h in range(ranks):
@@ -286,26 +286,25 @@
     return jnp.sum(jnp.where(spot, row, 0.0), axis=1, keepdims=True)
 
 
-def exchange_kernel(raws, *refs):
+def exchange_kernel(levels, *refs):
     (disp_hbm, load_hbm, conn_hbm, halo_hbm, grad_hbm, volume_hbm, moduli_hbm, owner_hbm) = refs[:8]
     (state_hbm, props_hbm, green_hbm, plane_hbm) = refs[8:12]
     residual, moved_out = refs[12:14]
-    (st, raw_send, raw_recv, ex_send, ex_recv, new_src, new_raw, props, green, plane) = refs[14:24]
-    buffers = refs[24:29]
-    (note_send, note_recv, mean_src, mean_raw, mean_stage, mean_all) = refs[29:35]
-    (halo_send, halo_recv, force_send, force_recv, strain_ref, onehot, forces, rows_i) = refs[35:43]
-    (disp, load, conn, halo, grad, volume, moduli, owner) = refs[43:51]
-    (source_vec, source_ref, order_vec, order_ref, got, load_sem, recv, sent) = refs[51:]
-    sources, ranks, rows = ex_recv.shape[:3]
-    groups, levels = ranks * rows, sources + raws
+    (st, trade_send, trade_recv, trade_new, raw_send, raw_recv, raw_new) = refs[14:21]
+    (mix_trade, mix_send, mix_recv, mix_new, got, props, green, plane) = refs[21:29]
+    buffers = refs[29:34]
+    (note_send, note_recv, mean_src, mean_raw, mean_mix, mean_far, stage, mean_all) = refs[34:42]
+    (halo_send, halo_recv, force_send, force_recv, mixed, strain_ref, onehot, forces, rows_i) = refs[42:51]
+    (disp, load, conn, halo, grad, volume, moduli, owner) = refs[51:59]
+    (source_vec, source_ref, order_vec, order_ref, load_sem, recv, sent) = refs[59:]
+    ranks, rows = trade_recv.shape[:2]
+    groups, half = ranks * rows, rows // 2
     own_nodes, elements, halos = disp.shape[1], conn.shape[1], halo.shape[1]
     me, mine = lax.axis_index("macro"), lax.axis_index("vox")
     my_row, my_side = me // ranks, me % ranks
     raw_side = (mine + ranks * groups - me) % ranks
-    R_PROPS, R_NOTE, R_HALO, R_FORCE, R_EX = range(5)
-    R_MEAN, R_GOT = R_EX + sources, R_EX + 2 * sources
-    R_RAW = R_GOT + levels
-    R_MRAW = R_RAW + raws
+    my_odd, my_pair = my_row % 2, my_row // 2
+    R_PROPS, R_NOTE, R_HALO, R_FORCE, R_TRADE, R_MEAN, R_RAW, R_MRAW, R_MIXT, R_MIX, R_MMIX, R_MFAR, R_GOT = range(13)
     f32 = jnp.float32
 
     def push(src, dst, kind, group, rank):
@@ -415,52 +414,74 @@
     def slab_of(slot):
         return st[:, jnp.clip(source_ref[0, slot], 0, elements - 1)]
 
-    def gather_trade(lv):
+    def expect(count, sem):
+        drain(got.at[pl.ds(0, count)], sem)
+
+    def gather_trade(low, stride, start, here, away):
         for o in range(ranks):
 
             def gather(i, carry, o=o):
-                slab = slab_of(lv * groups + ranks * i + (mine + o) % ranks)
+                slab = slab_of(low + ranks * (stride * i + start) + (mine + o) % ranks)
                 if o == 0:
-                    ex_recv[lv, mine, i] = slab
+                    here[mine, i] = slab
                 else:
-                    ex_send[lv, o - 1, i] = slab
+                    away[o - 1, i] = slab
                 return carry
 
-            lax.fori_loop(0, rows, gather, 0)
-
-    for lv in range(sources):
-        gather_trade(lv)
-    for q in range(raws):
-
-        def gather_raw(d, carry, q=q):
-            raw_send[q, d] = slab_of((sources + q) * groups + d)
+            lax.fori_loop(0, away.shape[1], gather, 0)
+
+    gather_trade(0, 1, 0, trade_recv, trade_send)
+    if levels > 1:
+
+        def gather_raw(d, carry):
+            raw_send[d] = slab_of(groups + d)
             return carry
 
         lax.fori_loop(0, groups, gather_raw, 0)
+    if levels > 2:
+        gather_trade(2 * groups, 2, 1 - my_odd, mix_recv, mix_trade)
+
+        def gather_mix(v, carry):
+            mix_send[v] = slab_of(2 * groups + ranks * (2 * (v // ranks) + my_odd) + v % ranks)
+            return carry
+
+        lax.fori_loop(0, groups // 2, gather_mix, 0)
     pl.semaphore_wait(barrier, total - 1)
 
     row_block = math.gcd(rows, 2)
 
-    def trade(lv):
-        for o in range(1, ranks):
-            push(ex_send.at[lv, o - 1], ex_recv.at[lv, mine], R_EX + lv, me, (mine + o) % ranks)
-
-    def send_raw(q, o):
+    def side_of(o):
         side = (mine + o) % ranks
+        return side, (side + ranks * groups - me) % ranks
+
+    def send_raw(o):
+        side, spot = side_of(o)
 
         def step(t, carry):
-            d = ranks * turn(t, rows, row_block, my_row) + (side + ranks * groups - me) % ranks
-            deliver(raw_send.at[q, d], raw_recv.at[q, mine, my_row], R_RAW + q, d, side)
+            d = ranks * turn(t, rows, row_block, my_row) + spot
+            deliver(raw_send.at[d], raw_recv.at[mine, my_row], R_RAW, d, side)
             return carry
 
         lax.fori_loop(0, rows, step, 0)
+
+    def send_mix(o):
+        side, spot = side_of(o)
+
+        def step(t, carry):
+            u = turn(t, half, 1, my_pair)
+            d = ranks * (2 * u + my_odd) + spot
+            deliver(mix_send.at[u * ranks + spot], mix_recv.at[mine, half + my_pair], R_MIX, d, side)
+            return carry
+
+        lax.fori_loop(0, half, step, 0)
 
     push(halo_send, halo_recv, R_HALO, (me + 1) % groups, mine)
     for o in range(1, ranks):
         push(props_hbm, props.at[mine], R_PROPS, me, (mine + o) % ranks)
-    trade(0)
-    if raws:
-        send_raw(0, 0)
+    for o in range(1, ranks):
+        push(trade_send.at[o - 1], trade_recv.at[mine], R_TRADE, me, (mine + o) % ranks)
+    if levels > 1:
+        send_raw(0)
 
     fetches[4].wait()
     fetches[5].wait()
@@ -503,9 +524,9 @@
         ]
         return parts[0] + (parts[1] + parts[2])
 
-    for q in range(raws):
-        held = strain_of(count_up(wide, 0) + (sources + q) * groups)
-        note = note + (pltpu.roll(held, 16 * q, 1) if q else held)
+    for lv in range(1, levels):
+        held = strain_of(count_up(wide, 0) + lv * groups)
+        note = note + pltpu.roll(held, 16 * lv, 1)
     for lv in range(levels):
         held = jnp.where(matched(count_up(wide, 0) + lv * groups), 1.0, 0.0)
         note = jnp.where(count_up(wide, 1) == 8 + lv, jnp.sum(held, axis=1, keepdims=True), note)
@@ -524,35 +545,66 @@
     if ranks > 1:
         drain(props.at[pl.ds(0, ranks - 1)], recv.at[R_PROPS])
 
-    def send_new(lv, low, high, turns):
+    def send_new(low, high, turns):
         def step(t, carry):
             i = turn(t, rows, row_block, my_row)
             for o in turns:
                 h = (mine + o) % ranks
-                deliver(new_src.at[lv, h, i], got.at[lv * groups + me], R_GOT + lv, ranks * i + mine, h)
+                deliver(trade_new.at[h, i], got.at[me], R_GOT, ranks * i + mine, h)
             return carry
 
         lax.fori_loop(low, high, step, 0)
 
+    def send_mixed(turns):
+        def step(t, carry):
+            u = turn(t, half, 1, my_pair)
+            for o in turns:
+                h = (mine + o) % ranks
+                spot = ranks * (2 * u + 1 - my_odd) + mine
+                push(mix_new.at[h, u], got.at[2 * groups + me], R_GOT + 2, spot, h)
+            return carry
+
+        lax.fori_loop(0, half, step, 0)
+
+    def give_back(new, first, count, low, kind, stride, start):
+        def step(i, carry):
+            for o in range(ranks):
+                h = (mine + o) % ranks
+                giver = ranks * (stride * i + start) + raw_side
+                deliver(new.at[h, first + i], got.at[low + giver], kind, me, h)
+            return carry
+
+        lax.fori_loop(0, count, step, 0)
+
+    def send_means(means, first, count, dst, kind, stride, start):
+        for i in range(count):
+            stage[first + i if count < rows else rows + i] = jnp.broadcast_to(
+                means[first + i : first + i + 1, :], (8, LANES)
+            )
+
+        def step(t, carry):
+            i = turn(t, count, math.gcd(count, 2), my_row * count // rows)
+            for h in range(ranks):
+                src = stage.at[first + i if count < rows else rows + i]
+                deliver(src, dst, kind, ranks * (stride * i + start) + raw_side, h)
+            return carry
+
+        lax.fori_loop(0, count, step, 0)
+
     near, far = range(1), range(1, ranks)
-    early = rows // 2 if raws else rows
-    for lv in range(sources):
-        ids = lv * groups + ranks * count_up((rows, LANES), 0) + mine
-        strain = strain_of(ids)
-        if ranks > 1:
-            drain(ex_recv.at[lv, pl.ds(0, ranks - 1)], recv.at[R_EX + lv])
-        if lv == 0:
-            for later in range(1, sources):
-                trade(later)
-            if raws:
-                for o in range(1, ranks):
-                    send_raw(0, o)
-        means = solve_rows(ex_recv.at[lv], strain, new_src.at[lv], props, green, plane, buffers)
-        mean_src[lv, mine] = means
-        for o in range(1, ranks):
-            push(mean_src.at[lv, mine], mean_src.at[lv, mine], R_MEAN + lv, me, (mine + o) % ranks)
-        if not raws:
-            send_new(lv, 0, rows, range(ranks))
+    early = rows // 2 if levels > 1 else rows
+    strain = strain_of(ranks * count_up((rows, LANES), 0) + mine)
+    if ranks > 1:
+        expect((ranks - 1) * rows, recv.at[R_TRADE])
+    if levels > 1:
+        for o in far:
+            send_raw(o)
+    means = solve_rows(trade_recv, strain, 0, trade_new, props, green, plane, buffers)
+    mean_src[mine] = means
+    for o in far:
+        push(mean_src.at[mine], mean_src.at[mine], R_MEAN, me, (mine + o) % ranks)
+    if levels == 1:
+        send_new(0, rows, range(ranks))
 
     drain(note_recv, recv.at[R_NOTE])
     flags = note_recv[:, 0, :]
@@ -580,57 +632,66 @@
     order_scalars = pltpu.make_async_copy(order_vec, order_ref, load_sem.at[12])
     order_scalars.start()
 
-    for q in range(raws):
-        drain(raw_recv.at[q], recv.at[R_RAW + q])
-        if q + 1 < raws:
-            for o in range(ranks):
-                send_raw(q + 1, o)
-        else:
-            for lv in range(sources):
-                send_new(lv, 0, rows, far)
-                send_new(lv, 0, early, near)
-        strain = pltpu.roll(note_recv[pl.ds(raw_side * rows, rows), 0, :], LANES - 16 * q, 1)
-        means = solve_rows(raw_recv.at[q], strain, new_raw.at[q], props, green, plane, buffers)
-        for i in range(rows):
-            mean_stage[q, i] = jnp.broadcast_to(means[i : i + 1, :], (8, LANES))
-
-        def send_back(t, carry, q=q):
-            i = turn(t, rows, row_block, my_row)
-            for h in range(ranks):
-                deliver(mean_stage.at[q, i], mean_raw.at[q, me], R_MRAW + q, ranks * i + raw_side, h)
-            return carry
-
-        lax.fori_loop(0, rows, send_back, 0)
-
-        def send_done(i, carry, q=q):
-            for o in range(ranks):
-                h = (mine + o) % ranks
-                spot = (sources + q) * groups + ranks * i + raw_side
-                deliver(new_raw.at[q, h, i], got.at[spot], R_GOT + sources + q, me, h)
-            return carry
-
-        lax.fori_loop(0, rows, send_done, 0)
-    for lv in range(sources):
-        send_new(lv, early, rows, near)
+    if levels > 1:
+        expect(groups, recv.at[R_RAW])
+        if levels > 2:
+            for o in far:
+                push(mix_trade.at[o - 1], mix_recv.at[mine, pl.ds(0, half)], R_MIXT, me, (mine + o) % ranks)
+                send_mix(o)
+            send_mix(0)
+        strain = note_recv[pl.ds(raw_side * rows, rows), 0, :]
+        means = solve_rows(raw_recv, strain, 16, raw_new, props, green, plane, buffers)
+        send_means(means, 0, rows, mean_raw.at[me], R_MRAW, 1, 0)
+        give_back(raw_new, 0, rows, groups, R_GOT + 1, 1, 0)
+        send_new(0, rows, far)
+        send_new(0, early, near)
+    if levels > 2:
+        mixed[...] = strain_of(2 * groups + ranks * (2 * count_up((8, LANES), 0) + 1 - my_odd) + mine)
+        mixed[...] = pltpu.roll(mixed[...], 32, 1)
+        for u in range(half):
+            mixed[half + u : half + u + 1, :] = note_recv[raw_side * rows + 2 * u + my_odd][0:1, :]
+        if ranks > 1:
+            expect((ranks - 1) * half, recv.at[R_MIXT])
+        expect(ranks * half, recv.at[R_MIX])
+        means = solve_rows(mix_recv, mixed[0:rows, :], 32, mix_new, props, green, plane, buffers)
+        mean_mix[mine] = means
+        for o in far:
+            push(mean_mix.at[mine], mean_mix.at[mine], R_MMIX, me, (mine + o) % ranks)
+        send_means(means, half, half, mean_far.at[my_pair * ranks + my_side], R_MFAR, 2, my_odd)
+        send_mixed(far)
+        give_back(mix_new, half, half, 2 * groups, R_GOT + 2, 2, my_odd)
+        send_mixed(near)
+    if levels > 1:
+        send_new(early, rows, near)
 
     fetches[9].wait()
     fetches[10].wait()
     fetches[11].wait()
-    for lv in range(sources):
-        if ranks > 1:
-            drain(mean_src.at[lv, pl.ds(0, ranks - 1)], recv.at[R_MEAN + lv])
-        for y in range(ranks):
-            mean_all[lv * groups + y * rows : lv * groups + (y + 1) * rows, :] = mean_src[lv, y]
-    for q in range(raws):
-        drain(mean_raw.at[q], recv.at[R_MRAW + q])
-        low = (sources + q) * groups
-        mean_all[low : low + groups, :] = mean_raw[q, :, 0, :]
     deep = (levels * groups, LANES)
     k = count_up(deep, 0)
     inside = k % groups
-    known = k - inside + jnp.where(
-        k < sources * groups, ranks * (inside % rows) + inside // rows, inside
-    )
+    known = ranks * (inside % rows) + inside // rows
+    if ranks > 1:
+        drain(mean_src.at[pl.ds(0, ranks - 1)], recv.at[R_MEAN])
+    for y in range(ranks):
+        mean_all[y * rows : (y + 1) * rows, :] = mean_src[y]
+    if levels > 1:
+        drain(mean_raw, recv.at[R_MRAW])
+        mean_all[groups : 2 * groups, :] = mean_raw[:, 0, :]
+        known = jnp.where(k < groups, known, k)
+    if levels > 2:
+        if ranks > 1:
+            drain(mean_mix.at[pl.ds(0, ranks - 1)], recv.at[R_MMIX])
+        drain(mean_far, recv.at[R_MFAR])
+        middle = 2 * groups + groups // 2
+        for y in range(ranks):
+            low = 2 * groups + y * half
+            mean_all[low : low + half, :] = mean_mix[y, 0:half, :]
+        mean_all[middle:, :] = mean_far[:, 0, :]
+        from_src = 2 * groups + ranks * (2 * (inside % half) + 1 - my_odd) + inside // half
+        v = inside - groups // 2
+        from_raw = 2 * groups + ranks * (2 * (v // ranks) + my_odd) + v % ranks
+        known = jnp.where(k < 2 * groups, known, jnp.where(k < middle, from_src, from_raw))
     match = jnp.where(matched(known), 1.0, 0.0).astype(jnp.bfloat16)
     mean_t = jnp.transpose(mean_all[...])[0:8, :]
     averaged = select_dot(mean_t, match, False)[:, 0:elements]
@@ -677,34 +738,40 @@
     drain(force_send, sent.at[R_FORCE])
     if ranks > 1:
         drain(props.at[pl.ds(0, ranks - 1)], sent.at[R_PROPS])
-    for lv in range(sources):
+    if ranks > 1:
+        drain(trade_send, sent.at[R_TRADE])
+        drain(mean_src.at[pl.ds(0, ranks - 1)], sent.at[R_MEAN])
+    settle(got.at[pl.ds(0, groups)], R_GOT, my_side == mine)
+    own = (2 * me) % ranks == mine
+    if levels > 1:
+        settle(raw_send, R_RAW, own)
+        settle(mean_raw, R_MRAW, own)
         if ranks > 1:
-            drain(ex_send.at[lv], sent.at[R_EX + lv])
-            drain(mean_src.at[lv, pl.ds(0, ranks - 1)], sent.at[R_MEAN + lv])
-        settle(got.at[pl.ds(0, groups)], R_GOT + lv, my_side == mine)
-    own = (2 * me) % ranks == mine
-    for q in range(raws):
-        settle(raw_send.at[q], R_RAW + q, own)
-        settle(mean_raw.at[q], R_MRAW + q, own)
+            expect((ranks - 1) * rows, sent.at[R_GOT + 1])
+    if levels > 2:
+        settle(mix_send, R_MIX, own)
+        settle(mean_far, R_MFAR, own)
         if ranks > 1:
-            drain(got.at[pl.ds(0, groups - rows)], sent.at[R_GOT + sources + q])
-
-
-def exchange(smalls, state, moduli, tables, levels, raws):
+            drain(mix_trade, sent.at[R_MIXT])
+            drain(mean_mix.at[pl.ds(0, ranks - 1)], sent.at[R_MMIX])
+        expect(ranks * half + (ranks - 1) * half, sent.at[R_GOT + 2])
+
+
+def exchange(smalls, state, moduli, tables, levels):
     groups, ranks = lax.axis_size("macro"), lax.axis_size("vox")
     rows = groups // ranks
     thickness = state.shape[2]
-    sources = levels - raws
+    half, extra, mix = rows // 2, min(levels - 1, 1), 1 if levels > 2 else 0
     nodes, corners, elements = smalls[0].shape[1], smalls[2].shape[0], smalls[2].shape[1]
     slab = (7, thickness, VOX_PLANE)
     hbm = pl.BlockSpec(memory_space=pltpu.HBM)
     vmem = pl.BlockSpec(memory_space=pltpu.VMEM)
     f32 = jnp.float32
-    kinds = 5 + 2 * sources + levels + 2 * raws
+    kinds = 13 + levels
     cells = levels * VOX_SIDE * rows * VOX_PLANE
     tile = pltpu.VMEM((8, LANES), f32)
     return pl.pallas_call(
-        functools.partial(exchange_kernel, raws),
+        functools.partial(exchange_kernel, levels),
         out_shape=[
             jax.ShapeDtypeStruct((3, nodes), f32),
             jax.ShapeDtypeStruct((7, RECV_AGG) + slab[1:], f32),
@@ -713,12 +780,17 @@
         out_specs=[vmem, vmem],
         scratch_shapes=[
             pltpu.VMEM(state.shape, f32),
-            pltpu.VMEM((max(raws, 1), groups) + slab, f32),
-            pltpu.VMEM((max(raws, 1), ranks, rows) + slab, f32),
-            pltpu.VMEM((sources, max(ranks - 1, 1), rows) + slab, f32),
-            pltpu.VMEM((sources, ranks, rows) + slab, f32),
-            pltpu.VMEM((sources, ranks, rows) + slab, f32),
-            pltpu.VMEM((max(raws, 1), ranks, rows) + slab, f32),
+            pltpu.VMEM((max(ranks - 1, 1), rows) + slab, f32),
+            pltpu.VMEM((ranks, rows) + slab, f32),
+            pltpu.VMEM((ranks, rows) + slab, f32),
+            pltpu.VMEM((groups if extra else 1,) + slab, f32),
+            pltpu.VMEM((ranks, rows if extra else 1) + slab, f32),
+            pltpu.VMEM((ranks, rows if extra else 1) + slab, f32),
+            pltpu.VMEM((max(ranks - 1, 1), half if mix else 1) + slab, f32),
+            pltpu.VMEM((groups // 2 if mix else 1,) + slab, f32),
+            pltpu.VMEM((ranks, rows if mix else 1) + slab, f32),
+            pltpu.VMEM((ranks, rows if mix else 1) + slab, f32),
+            pltpu.VMEM((levels * groups,) + slab, f32),
             pltpu.VMEM((ranks,) + moduli.shape, f32),
             pltpu.VMEM(tables[0].shape, f32),
             pltpu.VMEM(tables[1].shape, tables[1].dtype),
@@ -729,10 +801,13 @@
             pltpu.VMEM((6, HALF - 1, rows, VOX_PLANE), f32),
             pltpu.VMEM((groups, 8, LANES), f32),
             pltpu.VMEM((groups, 8, LANES), f32),
-            pltpu.VMEM((sources, ranks, rows, LANES), f32),
-            pltpu.VMEM((max(raws, 1), groups, 8, LANES), f32),
-            pltpu.VMEM((max(raws, 1), rows, 8, LANES), f32),
+            pltpu.VMEM((ranks, rows, LANES), f32),
+            pltpu.VMEM((groups, 8, LANES), f32),
+            pltpu.VMEM((ranks, rows, LANES), f32),
+            pltpu.VMEM((groups // 2, 8, LANES), f32),
+            pltpu.VMEM((2 * rows, 8, LANES), f32),
             pltpu.VMEM((levels * groups, LANES), f32),
+            tile,
             tile,
             tile,
             tile,
@@ -748,7 +823,6 @@
             pltpu.SMEM((1, LANES), jnp.int32),
             pltpu.VMEM((1, LANES), jnp.int32),
             pltpu.SMEM((1, LANES), jnp.int32),
-            pltpu.VMEM((levels * groups,) + slab, f32),
             pltpu.SemaphoreType.DMA((13,)),
             pltpu.SemaphoreType.DMA((kinds,)),
             pltpu.SemaphoreType.DMA((kinds,)),
@@ -780,7 +854,7 @@
     groups = lax.axis_size("macro")
     tables = (jnp.asarray(green_tables()), plane_tables())
     levels = (PLASTIC_MAX + groups - 1) // groups
-    raws = levels - 1
+    assert levels <= 3
     smalls = (
         displacement,
         load,
@@ -791,7 +865,7 @@
         elastic_moduli,
         new_owner[None, :],
     )
-    return tuple(exchange(smalls, state, micro_moduli, tables, levels, raws))
+    return tuple(exchange(smalls, state, micro_moduli, tables, levels))
 
 
 def solution(mesh):

time: 86.3 us -> 82.4 us (0.955)
  Pallas kernels: 81.2 us -> 77.8 us
    pallas_call x1, Pallas kernels: 81.2 us -> 77.8 us  [exchange(): pl.pallas_call(functools.partial(exchange_kernel, levels), out_shape=[jax...]
where the time goes in v3:
time: 82.4 us; the launch traced here: 82.2 us
  Pallas kernels  77.8 us (94%)
  local copies, waits for them, and re-layouts  3.79 us (5%)
    pallas_call x1, Pallas kernels, exchange(): pl.pallas_call(functools.partial(exchange_kernel, levels), out_shape=[jax...  77.8 us
    unnamed x2, local copies, waits for them, and re-layouts  3.79 us

profile of v3, /device:TPU:0, one launch (start us, length us, event | category | flops | bytes accessed | tf_op | source)
XLA Modules:
  0.0 82.2 jit_solution(5207905353393340832)
XLA Ops:
  0.6 77.8 %shard_map.140 = (f32[3,64]{1,0:T(4,128)}, f32[7,24,8,256]{3,2,1,0:T(8,128)}) custom-call(f32[3,64]{1,0:T(4,128)} %refs_0_.1, f32[3,64]{1,0:T(4,128)} %refs_1_.1, s32[8,64]{1,0:T(8,128)} %refs_2_.1, s32[1,16]{1,0:T(1,128)} %bitcast.3, f32[3,8,64]{2,1,0:T(8,128)} %refs_4_.1, f32[1,64]{1,0:T(1,128)} %bitcast.4, f32[2,64]{1,0:T(2,128)} %refs_6_.1, ...), custom_call_target="tpu_custom_call" | custom-call | flops 7247757312 | bytes 11010048 | tf_op jit(solution)/shard_map/pallas_call | solution.py:773
  78.5 1.2 %copy.17 = f32[3,64]{1,0:T(4,128)} copy(f32[3,64]{1,0:T(4,128)} %get-tuple-element.4) | data formatting | bytes 1536
  79.7 2.5 %copy.18 = f32[7,24,8,256]{3,2,1,0:T(8,128)} copy(f32[7,24,8,256]{3,2,1,0:T(8,128)} %get-tuple-element.5) | data formatting | bytes 2752512

commit v4 on v3

--- a/solution.py
+++ b/solution.py
@@ -138,7 +138,7 @@
     return stress, shape, (1.5 * two_mu) * factor, gain
 
 
-def solve_rows(pieces, strain, base, out, props, green, plane, buffers):
+def solve_rows(pieces, strain, base, out, props, green, plane, buffers, hook):
     stx, eps, work, cos_ref, sin_ref = buffers
     ranks, rows, _, thickness, _ = pieces.shape
 
@@ -152,6 +152,7 @@
         eps[c] = jnp.broadcast_to(strain[:, base + c : base + c + 1][None], (VOX_SIDE, rows, VOX_PLANE))
 
     def sweep(step, carry):
+        hook(step)
         for h in range(ranks):
 
             def law(place, inner, h=h):
@@ -289,14 +290,14 @@
 def exchange_kernel(levels, *refs):
     (disp_hbm, load_hbm, conn_hbm, halo_hbm, grad_hbm, volume_hbm, moduli_hbm, owner_hbm) = refs[:8]
     (state_hbm, props_hbm, green_hbm, plane_hbm) = refs[8:12]
-    residual, moved_out = refs[12:14]
-    (st, trade_send, trade_recv, trade_new, raw_send, raw_recv, raw_new) = refs[14:21]
-    (mix_trade, mix_send, mix_recv, mix_new, got, props, green, plane) = refs[21:29]
+    residual_out, got, order_out = refs[12:15]
+    (st, trade_send, trade_recv, trade_new, raw_send, raw_recv, raw_new) = refs[15:22]
+    (mix_trade, mix_send, mix_recv, mix_new, props, green, plane) = refs[22:29]
     buffers = refs[29:34]
     (note_send, note_recv, mean_src, mean_raw, mean_mix, mean_far, stage, mean_all) = refs[34:42]
     (halo_send, halo_recv, force_send, force_recv, mixed, strain_ref, onehot, forces, rows_i) = refs[42:51]
     (disp, load, conn, halo, grad, volume, moduli, owner) = refs[51:59]
-    (source_vec, source_ref, order_vec, order_ref, load_sem, recv, sent) = refs[59:]
+    (source_vec, source_ref, order_vec, residual, load_sem, recv, sent) = refs[59:]
     ranks, rows = trade_recv.shape[:2]
     groups, half = ranks * rows, rows // 2
     own_nodes, elements, halos = disp.shape[1], conn.shape[1], halo.shape[1]
@@ -545,12 +546,15 @@
     if ranks > 1:
         drain(props.at[pl.ds(0, ranks - 1)], recv.at[R_PROPS])
 
+    def send_row(t, turns):
+        i = turn(t, rows, row_block, my_row)
+        for o in turns:
+            h = (mine + o) % ranks
+            deliver(trade_new.at[h, i], got.at[me], R_GOT, ranks * i + mine, h)
+
     def send_new(low, high, turns):
         def step(t, carry):
-            i = turn(t, rows, row_block, my_row)
-            for o in turns:
-                h = (mine + o) % ranks
-                deliver(trade_new.at[h, i], got.at[me], R_GOT, ranks * i + mine, h)
+            send_row(t, turns)
             return carry
 
         lax.fori_loop(low, high, step, 0)
@@ -592,14 +596,35 @@
         lax.fori_loop(0, count, step, 0)
 
     near, far = range(1), range(1, ranks)
-    early = rows // 2 if levels > 1 else rows
+
+    def trade_mix():
+        for o in far:
+            push(mix_trade.at[o - 1], mix_recv.at[mine, pl.ds(0, half)], R_MIXT, me, (mine + o) % ranks)
+
+    def first_hook(step):
+        if levels > 2:
+            pl.when(step == SWEEPS - 1)(trade_mix)
+
+    def second_hook(step):
+        if levels > 2:
+
+            @pl.when(step >= SWEEPS - 2)
+            def _():
+                low = 2 * (step - (SWEEPS - 2))
+                send_row(low, far)
+                send_row(low + 1, far)
+
+    def third_hook(step):
+        send_row(2 * step, near)
+        send_row(2 * step + 1, near)
+
     strain = strain_of(ranks * count_up((rows, LANES), 0) + mine)
     if ranks > 1:
         expect((ranks - 1) * rows, recv.at[R_TRADE])
     if levels > 1:
         for o in far:
             send_raw(o)
-    means = solve_rows(trade_recv, strain, 0, trade_new, props, green, plane, buffers)
+    means = solve_rows(trade_recv, strain, 0, trade_new, props, green, plane, buffers, first_hook)
     mean_src[mine] = means
     for o in far:
         push(mean_src.at[mine], mean_src.at[mine], R_MEAN, me, (mine + o) % ranks)
@@ -629,22 +654,22 @@
         picks = picks + jnp.sum(jnp.where(chosen, lv * groups + giver, 0.0), axis=0, keepdims=True)
         place = place + held
     order_vec[...] = picks.astype(jnp.int32)
-    order_scalars = pltpu.make_async_copy(order_vec, order_ref, load_sem.at[12])
-    order_scalars.start()
+    give_order = pltpu.make_async_copy(order_vec, order_out, load_sem.at[12])
+    give_order.start()
 
     if levels > 1:
         expect(groups, recv.at[R_RAW])
         if levels > 2:
-            for o in far:
-                push(mix_trade.at[o - 1], mix_recv.at[mine, pl.ds(0, half)], R_MIXT, me, (mine + o) % ranks)
+            for o in range(ranks - 1, -1, -1):
                 send_mix(o)
-            send_mix(0)
         strain = note_recv[pl.ds(raw_side * rows, rows), 0, :]
-        means = solve_rows(raw_recv, strain, 16, raw_new, props, green, plane, buffers)
+        means = solve_rows(raw_recv, strain, 16, raw_new, props, green, plane, buffers, second_hook)
         send_means(means, 0, rows, mean_raw.at[me], R_MRAW, 1, 0)
         give_back(raw_new, 0, rows, groups, R_GOT + 1, 1, 0)
-        send_new(0, rows, far)
-        send_new(0, early, near)
+        if levels > 2:
+            send_new(half, rows, far)
+        else:
+            send_new(0, rows, range(ranks))
     if levels > 2:
         mixed[...] = strain_of(2 * groups + ranks * (2 * count_up((8, LANES), 0) + 1 - my_odd) + mine)
         mixed[...] = pltpu.roll(mixed[...], 32, 1)
@@ -653,17 +678,13 @@
         if ranks > 1:
             expect((ranks - 1) * half, recv.at[R_MIXT])
         expect(ranks * half, recv.at[R_MIX])
-        means = solve_rows(mix_recv, mixed[0:rows, :], 32, mix_new, props, green, plane, buffers)
+        means = solve_rows(mix_recv, mixed[0:rows, :], 32, mix_new, props, green, plane, buffers, third_hook)
         mean_mix[mine] = means
         for o in far:
             push(mean_mix.at[mine], mean_mix.at[mine], R_MMIX, me, (mine + o) % ranks)
         send_means(means, half, half, mean_far.at[my_pair * ranks + my_side], R_MFAR, 2, my_odd)
         send_mixed(far)
         give_back(mix_new, half, half, 2 * groups, R_GOT + 2, 2, my_odd)
-        send_mixed(near)
-    if levels > 1:
-        send_new(early, rows, near)
-
     fetches[9].wait()
     fetches[10].wait()
     fetches[11].wait()
@@ -717,22 +738,21 @@
         assembled = assembled + select_dot(forces[a], onehot[a], True)
     force_send[...] = assembled
     push(force_send, force_recv, R_FORCE, (me + groups - 1) % groups, mine)
+    if levels > 2:
+        send_mixed(near)
     drain(force_recv, recv.at[R_FORCE])
     lane8 = count_up((8, LANES), 1)
     beyond = (lane8 >= own_nodes) & (lane8 < own_nodes + halos)
     back = jnp.where(beyond, force_recv[...], 0.0)
     total_force = assembled + select_dot(back, halo_match, True)
     residual[...] = total_force[0:3, 0:own_nodes] - load[...]
+    give_residual = pltpu.make_async_copy(residual, residual_out, load_sem.at[13])
+    give_residual.start()
 
     for lv in range(levels):
         drain(got.at[pl.ds(lv * groups, groups)], recv.at[R_GOT + lv])
-    order_scalars.wait()
-
-    def place_row(j, carry):
-        moved_out[:, j] = got[jnp.clip(order_ref[0, j], 0, levels * groups - 1)]
-        return carry
-
-    lax.fori_loop(0, moved_out.shape[1], place_row, 0)
+    give_order.wait()
+    give_residual.wait()
     drain(note_send.at[pl.ds(0, groups - 1)], sent.at[R_NOTE])
     drain(halo_send, sent.at[R_HALO])
     drain(force_send, sent.at[R_FORCE])
@@ -765,7 +785,6 @@
     nodes, corners, elements = smalls[0].shape[1], smalls[2].shape[0], smalls[2].shape[1]
     slab = (7, thickness, VOX_PLANE)
     hbm = pl.BlockSpec(memory_space=pltpu.HBM)
-    vmem = pl.BlockSpec(memory_space=pltpu.VMEM)
     f32 = jnp.float32
     kinds = 13 + levels
     cells = levels * VOX_SIDE * rows * VOX_PLANE
@@ -774,10 +793,11 @@
         functools.partial(exchange_kernel, levels),
         out_shape=[
             jax.ShapeDtypeStruct((3, nodes), f32),
-            jax.ShapeDtypeStruct((7, RECV_AGG) + slab[1:], f32),
+            jax.ShapeDtypeStruct((levels * groups,) + slab, f32),
+            jax.ShapeDtypeStruct((1, LANES), jnp.int32),
         ],
         in_specs=[hbm] * (len(smalls) + 2 + len(tables)),
-        out_specs=[vmem, vmem],
+        out_specs=[hbm] * 3,
         scratch_shapes=[
             pltpu.VMEM(state.shape, f32),
             pltpu.VMEM((max(ranks - 1, 1), rows) + slab, f32),
@@ -790,7 +810,6 @@
             pltpu.VMEM((groups // 2 if mix else 1,) + slab, f32),
             pltpu.VMEM((ranks, rows if mix else 1) + slab, f32),
             pltpu.VMEM((ranks, rows if mix else 1) + slab, f32),
-            pltpu.VMEM((levels * groups,) + slab, f32),
             pltpu.VMEM((ranks,) + moduli.shape, f32),
             pltpu.VMEM(tables[0].shape, f32),
             pltpu.VMEM(tables[1].shape, tables[1].dtype),
@@ -822,8 +841,8 @@
             pltpu.VMEM((1, LANES), jnp.int32),
             pltpu.SMEM((1, LANES), jnp.int32),
             pltpu.VMEM((1, LANES), jnp.int32),
-            pltpu.SMEM((1, LANES), jnp.int32),
-            pltpu.SemaphoreType.DMA((13,)),
+            pltpu.VMEM((3, nodes), f32),
+            pltpu.SemaphoreType.DMA((14,)),
             pltpu.SemaphoreType.DMA((kinds,)),
             pltpu.SemaphoreType.DMA((kinds,)),
         ],
@@ -836,6 +855,49 @@
             transcendentals=SWEEPS * cells,
         ),
     )(*smalls, state, moduli, *tables)
+
+
+def pick_kernel(order_hbm, got, residual, residual_out, moved, order_ref, held, load_sem, slot_sem, out_sem):
+    count, slots = held.shape[0], got.shape[0]
+    fetch = pltpu.make_async_copy(order_hbm, order_ref, load_sem.at[0])
+    fetch.start()
+    keep = pltpu.make_async_copy(residual, residual_out, load_sem.at[1])
+    keep.start()
+    fetch.wait()
+
+    def take(j):
+        slot = jnp.clip(order_ref[0, j], 0, slots - 1)
+        return pltpu.make_async_copy(got.at[slot], held.at[j], slot_sem.at[j])
+
+    for j in range(count):
+        take(j).start()
+    for j in range(count):
+        drain(held.at[j], slot_sem.at[j])
+        pltpu.make_async_copy(held.at[j], moved.at[:, j], out_sem).start()
+    keep.wait()
+    drain(held, out_sem)
+
+
+def pick_rows(order, got, residual):
+    slab = got.shape[1:]
+    hbm = pl.BlockSpec(memory_space=pltpu.HBM)
+    return pl.pallas_call(
+        pick_kernel,
+        out_shape=[
+            jax.ShapeDtypeStruct(residual.shape, jnp.float32),
+            jax.ShapeDtypeStruct(slab[:1] + (RECV_AGG,) + slab[1:], jnp.float32),
+        ],
+        in_specs=[hbm] * 3,
+        out_specs=[hbm] * 2,
+        scratch_shapes=[
+            pltpu.SMEM(order.shape, jnp.int32),
+            pltpu.VMEM((RECV_AGG,) + slab, jnp.float32),
+            pltpu.SemaphoreType.DMA((2,)),
+            pltpu.SemaphoreType.DMA((RECV_AGG,)),
+            pltpu.SemaphoreType.DMA,
+        ],
+        compiler_params=pltpu.CompilerParams(vmem_limit_bytes=63 * 2**20),
+    )(order, got, residual)
 
 
 def local(
@@ -854,7 +916,7 @@
     groups = lax.axis_size("macro")
     tables = (jnp.asarray(green_tables()), plane_tables())
     levels = (PLASTIC_MAX + groups - 1) // groups
-    assert levels <= 3
+    assert levels <= 3 and groups // lax.axis_size("vox") == 2 * SWEEPS
     smalls = (
         displacement,
         load,
@@ -865,7 +927,8 @@
         elastic_moduli,
         new_owner[None, :],
     )
-    return tuple(exchange(smalls, state, micro_moduli, tables, levels))
+    residual, got, order = exchange(smalls, state, micro_moduli, tables, levels)
+    return tuple(pick_rows(order, got, residual))
 
 
 def solution(mesh):

time: 82.4 us -> 80.2 us (0.973)
  local copies, waits for them, and re-layouts: 3.79 us -> 0 us
  Pallas kernels: 77.8 us -> 79.3 us
    unnamed x2 -> x0, local copies, waits for them, and re-layouts: 3.79 us -> none
    pallas_call x0 -> x1, Pallas kernels: none -> 2.87 us  [pick_rows(): pl.pallas_call(pick_kernel, out_shape=[jax.ShapeDtypeStruct(residual.shap...]
    pallas_call x1, Pallas kernels: 77.8 us -> 76.4 us  [exchange(): pl.pallas_call(functools.partial(exchange_kernel, levels), out_shape=[jax...]
where the time goes in v4:
time: 80.2 us; the launch traced here: 80 us
  Pallas kernels  79.3 us (99%)
    pallas_call x1, Pallas kernels, exchange(): pl.pallas_call(functools.partial(exchange_kernel, levels), out_shape=[jax...  76.4 us
    pallas_call x1, Pallas kernels, pick_rows(): pl.pallas_call(pick_kernel, out_shape=[jax.ShapeDtypeStruct(residual.shap...  2.87 us

profile of v4, /device:TPU:0, one launch (start us, length us, event | category | flops | bytes accessed | tf_op | source)
XLA Modules:
  0.0 80.0 jit_solution(10503001732384693532)
XLA Ops:
  0.6 76.4 %shard_map.140 = (f32[3,64]{1,0:T(4,128)}, f32[48,7,8,256]{3,2,1,0:T(8,128)}, s32[1,128]{1,0:T(1,128)}) custom-call(f32[3,64]{1,0:T(4,128)} %refs_0_.1, f32[3,64]{1,0:T(4,128)} %refs_1_.1, s32[8,64]{1,0:T(8,128)} %refs_2_.1, s32[1,16]{1,0:T(1,128)} %bitcast.3, f32[3,8,64]{2,1,0:T(8,128)} %refs_4_.1, f32[1,64]{1,0:T(1,128)} %bitcast.4, f32[2,64]{1,0:T(2,128)} %refs_6_.1, ...), custom_call_target="tpu_custom_call" | custom-call | flops 7247757312 | bytes 11010048 | tf_op jit(solution)/shard_map/pallas_call | solution.py:792
  77.1 2.9 %shard_map.141 = (f32[3,64]{1,0:T(4,128)}, f32[7,24,8,256]{3,2,1,0:T(8,128)}) custom-call(s32[1,128]{1,0:T(1,128)} %get-tuple-element.5.order_hbm, f32[48,7,8,256]{3,2,1,0:T(8,128)} %get-tuple-element.6.got, f32[3,64]{1,0:T(4,128)} %get-tuple-element.7.residual), custom_call_target="tpu_custom_call" | custom-call | tf_op jit(solution)/shard_map/pallas_call | solution.py:884

commit v5 on v4

--- a/solution.py
+++ b/solution.py
@@ -116,31 +116,40 @@
     return dot(high, table_ref[first]) + (dot(high, table_ref[first + 1]) + dot(low, table_ref[first]))
 
 
-def voxel_law(strain, state, props, row):
-    lam, mu = props[0, row, :], props[1, row, :]
-    yield_base, harden = props[2, row, :], props[3, row, :]
-    two_mu, three_mu = 2.0 * mu, 3.0 * mu
-    stiff_inv = 1.0 / (three_mu + harden)
-    bulk = lam + two_mu * (1.0 / 3.0)
+def prepare_law(props, laws):
+    for h in range(props.shape[0]):
+        lam, mu, yield_base, harden = [props[h, n] for n in range(4)]
+        stiff_inv = 1.0 / (3.0 * mu + harden)
+        laws[h, 0] = 2.0 * mu
+        laws[h, 1] = lam + 2.0 * mu * (1.0 / 3.0)
+        laws[h, 2] = yield_base * (0.5 / mu)
+        laws[h, 3] = harden * (0.5 / mu)
+        laws[h, 4] = stiff_inv
+        laws[h, 5] = 3.0 * mu * stiff_inv
+
+
+def voxel_law(strain, state, laws, row):
+    two_mu, bulk, yield_base, harden, stiff_inv, soften = [laws[n, row, :] for n in range(6)]
     elastic = [strain[c] - state[c] for c in range(6)]
     trace = elastic[0] + elastic[1] + elastic[2]
     third = trace * (1.0 / 3.0)
     shape = [elastic[c] - third for c in range(3)] + elastic[3:]
     normal = shape[0] * shape[0] + shape[1] * shape[1] + shape[2] * shape[2]
     shear = shape[3] * shape[3] + shape[4] * shape[4] + shape[5] * shape[5]
-    equivalent = two_mu * jnp.sqrt(1.5 * (normal + 2.0 * shear))
+    squared = jnp.maximum(1.5 * normal + 3.0 * shear, 1e-30)
+    inverse = lax.rsqrt(squared)
     strength = yield_base + harden * state[6]
-    gain = jnp.maximum(equivalent - strength, 0.0) * stiff_inv
-    factor = gain / jnp.maximum(equivalent, strength)
-    keep = two_mu * (1.0 - three_mu * factor)
+    share = jnp.maximum(1.0 - strength * inverse, 0.0)
+    keep = two_mu * (1.0 - soften * share)
     pressure = bulk * trace
     stress = [pressure + keep * shape[c] for c in range(3)] + [keep * shape[c] for c in range(3, 6)]
-    return stress, shape, (1.5 * two_mu) * factor, gain
-
-
-def solve_rows(pieces, strain, base, out, props, green, plane, buffers, hook):
+    return stress, shape, (two_mu * stiff_inv) * share, squared * inverse
+
+
+def solve_rows(pieces, strain, base, out, laws, green, plane, buffers, hook):
     stx, eps, work, cos_ref, sin_ref = buffers
     ranks, rows, _, thickness, _ = pieces.shape
+    batch = math.gcd(thickness, 4)
 
     def bring(c, carry):
         for h in range(ranks):
@@ -155,16 +164,18 @@
         hook(step)
         for h in range(ranks):
 
-            def law(place, inner, h=h):
-                x = h * thickness + place
-                strain = [eps[c, x] for c in range(6)]
-                state = [stx[c, x] for c in range(7)]
-                stress = voxel_law(strain, state, props.at[h], pl.ds(place, 1))[0]
-                for c in range(6):
-                    work[c, x] = stress[c]
+            def law(step, inner, h=h):
+                for part in range(batch):
+                    place = step * batch + part
+                    x = h * thickness + place
+                    strain = [eps[c, x] for c in range(6)]
+                    state = [stx[c, x] for c in range(7)]
+                    stress = voxel_law(strain, state, laws.at[h], pl.ds(place, 1))[0]
+                    for c in range(6):
+                        work[c, x] = stress[c]
                 return inner
 
-            lax.fori_loop(0, thickness, law, 0)
+            lax.fori_loop(0, thickness // batch, law, 0)
 
         def forward(c, inner):
             field = [work[c, x] for x in range(VOX_SIDE)]
@@ -235,10 +246,10 @@
             x = h * thickness + place
             strain = [eps[c, x] for c in range(6)]
             state = [stx[c, x] for c in range(7)]
-            stress, shape, scale, gain = voxel_law(strain, state, props.at[h], pl.ds(place, 1))
+            stress, shape, gain, size = voxel_law(strain, state, laws.at[h], pl.ds(place, 1))
             for c in range(6):
-                stx[c, x] = state[c] + scale * shape[c]
-            stx[6, x] = state[6] + gain
+                stx[c, x] = state[c] + (1.5 * gain) * shape[c]
+            stx[6, x] = state[6] + gain * size
             return tuple(totals[c] + stress[c] for c in range(6))
 
         totals = lax.fori_loop(0, thickness, finish, totals)
@@ -297,7 +308,7 @@
     (note_send, note_recv, mean_src, mean_raw, mean_mix, mean_far, stage, mean_all) = refs[34:42]
     (halo_send, halo_recv, force_send, force_recv, mixed, strain_ref, onehot, forces, rows_i) = refs[42:51]
     (disp, load, conn, halo, grad, volume, moduli, owner) = refs[51:59]
-    (source_vec, source_ref, order_vec, residual, load_sem, recv, sent) = refs[59:]
+    (source_vec, source_ref, order_vec, residual, laws, load_sem, recv, sent) = refs[59:]
     ranks, rows = trade_recv.shape[:2]
     groups, half = ranks * rows, rows // 2
     own_nodes, elements, halos = disp.shape[1], conn.shape[1], halo.shape[1]
@@ -418,8 +429,8 @@
     def expect(count, sem):
         drain(got.at[pl.ds(0, count)], sem)
 
-    def gather_trade(low, stride, start, here, away):
-        for o in range(ranks):
+    def gather_trade(low, stride, start, here, away, turns):
+        for o in turns:
 
             def gather(i, carry, o=o):
                 slab = slab_of(low + ranks * (stride * i + start) + (mine + o) % ranks)
@@ -431,7 +442,7 @@
 
             lax.fori_loop(0, away.shape[1], gather, 0)
 
-    gather_trade(0, 1, 0, trade_recv, trade_send)
+    gather_trade(0, 1, 0, trade_recv, trade_send, range(1, ranks))
     if levels > 1:
 
         def gather_raw(d, carry):
@@ -439,14 +450,6 @@
             return carry
 
         lax.fori_loop(0, groups, gather_raw, 0)
-    if levels > 2:
-        gather_trade(2 * groups, 2, 1 - my_odd, mix_recv, mix_trade)
-
-        def gather_mix(v, carry):
-            mix_send[v] = slab_of(2 * groups + ranks * (2 * (v // ranks) + my_odd) + v % ranks)
-            return carry
-
-        lax.fori_loop(0, groups // 2, gather_mix, 0)
     pl.semaphore_wait(barrier, total - 1)
 
     row_block = math.gcd(rows, 2)
@@ -483,6 +486,15 @@
         push(trade_send.at[o - 1], trade_recv.at[mine], R_TRADE, me, (mine + o) % ranks)
     if levels > 1:
         send_raw(0)
+    gather_trade(0, 1, 0, trade_recv, trade_send, range(1))
+    if levels > 2:
+        gather_trade(2 * groups, 2, 1 - my_odd, mix_recv, mix_trade, range(ranks))
+
+        def gather_mix(v, carry):
+            mix_send[v] = slab_of(2 * groups + ranks * (2 * (v // ranks) + my_odd) + v % ranks)
+            return carry
+
+        lax.fori_loop(0, groups // 2, gather_mix, 0)
 
     fetches[4].wait()
     fetches[5].wait()
@@ -545,6 +557,7 @@
     fetches[8].wait()
     if ranks > 1:
         drain(props.at[pl.ds(0, ranks - 1)], recv.at[R_PROPS])
+    prepare_law(props, laws)
 
     def send_row(t, turns):
         i = turn(t, rows, row_block, my_row)
@@ -603,6 +616,7 @@
 
     def first_hook(step):
         if levels > 2:
+            pl.when(step == SWEEPS - 2)(lambda: send_mix(0))
             pl.when(step == SWEEPS - 1)(trade_mix)
 
     def second_hook(step):
@@ -615,8 +629,9 @@
                 send_row(low + 1, far)
 
     def third_hook(step):
-        send_row(2 * step, near)
-        send_row(2 * step + 1, near)
+        @pl.when(step < SWEEPS // 2)
+        def _():
+            send_new(half * step, half * step + half, near)
 
     strain = strain_of(ranks * count_up((rows, LANES), 0) + mine)
     if ranks > 1:
@@ -624,7 +639,7 @@
     if levels > 1:
         for o in far:
             send_raw(o)
-    means = solve_rows(trade_recv, strain, 0, trade_new, props, green, plane, buffers, first_hook)
+    means = solve_rows(trade_recv, strain, 0, trade_new, laws, green, plane, buffers, first_hook)
     mean_src[mine] = means
     for o in far:
         push(mean_src.at[mine], mean_src.at[mine], R_MEAN, me, (mine + o) % ranks)
@@ -660,10 +675,10 @@
     if levels > 1:
         expect(groups, recv.at[R_RAW])
         if levels > 2:
-            for o in range(ranks - 1, -1, -1):
+            for o in far:
                 send_mix(o)
         strain = note_recv[pl.ds(raw_side * rows, rows), 0, :]
-        means = solve_rows(raw_recv, strain, 16, raw_new, props, green, plane, buffers, second_hook)
+        means = solve_rows(raw_recv, strain, 16, raw_new, laws, green, plane, buffers, second_hook)
         send_means(means, 0, rows, mean_raw.at[me], R_MRAW, 1, 0)
         give_back(raw_new, 0, rows, groups, R_GOT + 1, 1, 0)
         if levels > 2:
@@ -678,13 +693,14 @@
         if ranks > 1:
             expect((ranks - 1) * half, recv.at[R_MIXT])
         expect(ranks * half, recv.at[R_MIX])
-        means = solve_rows(mix_recv, mixed[0:rows, :], 32, mix_new, props, green, plane, buffers, third_hook)
+        means = solve_rows(mix_recv, mixed[0:rows, :], 32, mix_new, laws, green, plane, buffers, third_hook)
         mean_mix[mine] = means
         for o in far:
             push(mean_mix.at[mine], mean_mix.at[mine], R_MMIX, me, (mine + o) % ranks)
         send_means(means, half, half, mean_far.at[my_pair * ranks + my_side], R_MFAR, 2, my_odd)
         send_mixed(far)
         give_back(mix_new, half, half, 2 * groups, R_GOT + 2, 2, my_odd)
+        send_mixed(near)
     fetches[9].wait()
     fetches[10].wait()
     fetches[11].wait()
@@ -738,8 +754,6 @@
         assembled = assembled + select_dot(forces[a], onehot[a], True)
     force_send[...] = assembled
     push(force_send, force_recv, R_FORCE, (me + groups - 1) % groups, mine)
-    if levels > 2:
-        send_mixed(near)
     drain(force_recv, recv.at[R_FORCE])
     lane8 = count_up((8, LANES), 1)
     beyond = (lane8 >= own_nodes) & (lane8 < own_nodes + halos)
@@ -842,6 +856,7 @@
             pltpu.SMEM((1, LANES), jnp.int32),
             pltpu.VMEM((1, LANES), jnp.int32),
             pltpu.VMEM((3, nodes), f32),
+            pltpu.VMEM((ranks, 6) + moduli.shape[1:], f32),
             pltpu.SemaphoreType.DMA((14,)),
             pltpu.SemaphoreType.DMA((kinds,)),
             pltpu.SemaphoreType.DMA((kinds,)),

time: 80.2 us -> 76.4 us (0.953)
  Pallas kernels: 79.3 us -> 75.6 us
    pallas_call x1, Pallas kernels: 76.4 us -> 72.7 us  [exchange(): pl.pallas_call(functools.partial(exchange_kernel, levels), out_shape=[jax...]
where the time goes in v5:
time: 76.4 us; the launch traced here: 76.2 us
  Pallas kernels  75.6 us (99%)
    pallas_call x1, Pallas kernels, exchange(): pl.pallas_call(functools.partial(exchange_kernel, levels), out_shape=[jax...  72.7 us
    pallas_call x1, Pallas kernels, pick_rows(): pl.pallas_call(pick_kernel, out_shape=[jax.ShapeDtypeStruct(residual.shap...  2.87 us

profile of v5, /device:TPU:0, one launch (start us, length us, event | category | flops | bytes accessed | tf_op | source)
XLA Modules:
  0.0 76.2 jit_solution(3225483132636885942)
XLA Ops:
  0.6 72.7 %shard_map.140 = (f32[3,64]{1,0:T(4,128)}, f32[48,7,8,256]{3,2,1,0:T(8,128)}, s32[1,128]{1,0:T(1,128)}) custom-call(f32[3,64]{1,0:T(4,128)} %refs_0_.1, f32[3,64]{1,0:T(4,128)} %refs_1_.1, s32[8,64]{1,0:T(8,128)} %refs_2_.1, s32[1,16]{1,0:T(1,128)} %bitcast.3, f32[3,8,64]{2,1,0:T(8,128)} %refs_4_.1, f32[1,64]{1,0:T(1,128)} %bitcast.4, f32[2,64]{1,0:T(2,128)} %refs_6_.1, ...), custom_call_target="tpu_custom_call" | custom-call | flops 7247757312 | bytes 11010048 | tf_op jit(solution)/shard_map/pallas_call | solution.py:806
  73.4 2.9 %shard_map.141 = (f32[3,64]{1,0:T(4,128)}, f32[7,24,8,256]{3,2,1,0:T(8,128)}) custom-call(s32[1,128]{1,0:T(1,128)} %get-tuple-element.5.order_hbm, f32[48,7,8,256]{3,2,1,0:T(8,128)} %get-tuple-element.6.got, f32[3,64]{1,0:T(4,128)} %get-tuple-element.7.residual), custom_call_target="tpu_custom_call" | custom-call | tf_op jit(solution)/shard_map/pallas_call | solution.py:899

commit v6 on v5

--- a/solution.py
+++ b/solution.py
@@ -544,7 +544,7 @@
         held = jnp.where(matched(count_up(wide, 0) + lv * groups), 1.0, 0.0)
         note = jnp.where(count_up(wide, 1) == 8 + lv, jnp.sum(held, axis=1, keepdims=True), note)
     for d in range(groups):
-        note_send[d] = jnp.broadcast_to(note[d : d + 1, :], (8, LANES))
+        note_send[d] = note[d : d + 1, :]
 
     def send_note(t, carry):
         d = turn(t, groups, math.gcd(groups, 4), me)
@@ -595,9 +595,7 @@
 
     def send_means(means, first, count, dst, kind, stride, start):
         for i in range(count):
-            stage[first + i if count < rows else rows + i] = jnp.broadcast_to(
-                means[first + i : first + i + 1, :], (8, LANES)
-            )
+            stage[first + i if count < rows else rows + i] = means[first + i : first + i + 1, :]
 
         def step(t, carry):
             i = turn(t, count, math.gcd(count, 2), my_row * count // rows)
@@ -832,13 +830,13 @@
             pltpu.VMEM((6, VOX_SIDE, rows, VOX_PLANE), f32),
             pltpu.VMEM((6, HALF + 1, rows, VOX_PLANE), f32),
             pltpu.VMEM((6, HALF - 1, rows, VOX_PLANE), f32),
-            pltpu.VMEM((groups, 8, LANES), f32),
-            pltpu.VMEM((groups, 8, LANES), f32),
+            pltpu.VMEM((groups, 1, LANES), f32),
+            pltpu.VMEM((groups, 1, LANES), f32),
             pltpu.VMEM((ranks, rows, LANES), f32),
-            pltpu.VMEM((groups, 8, LANES), f32),
+            pltpu.VMEM((groups, 1, LANES), f32),
             pltpu.VMEM((ranks, rows, LANES), f32),
-            pltpu.VMEM((groups // 2, 8, LANES), f32),
-            pltpu.VMEM((2 * rows, 8, LANES), f32),
+            pltpu.VMEM((groups // 2, 1, LANES), f32),
+            pltpu.VMEM((2 * rows, 1, LANES), f32),
             pltpu.VMEM((levels * groups, LANES), f32),
             tile,
             tile,

time: 76.4 us -> 75.5 us (0.988)
  Pallas kernels: 75.6 us -> 74.6 us
    pallas_call x1, Pallas kernels: 72.7 us -> 71.8 us  [exchange(): pl.pallas_call(functools.partial(exchange_kernel, levels), out_shape=[jax...]
where the time goes in v6:
time: 75.5 us; the launch traced here: 75.3 us
  Pallas kernels  74.6 us (99%)
    pallas_call x1, Pallas kernels, exchange(): pl.pallas_call(functools.partial(exchange_kernel, levels), out_shape=[jax...  71.8 us
    pallas_call x1, Pallas kernels, pick_rows(): pl.pallas_call(pick_kernel, out_shape=[jax.ShapeDtypeStruct(residual.shap...  2.87 us

profile of v6, /device:TPU:0, one launch (start us, length us, event | category | flops | bytes accessed | tf_op | source)
XLA Modules:
  0.0 75.3 jit_solution(17854005103748248658)
XLA Ops:
  0.6 71.8 %shard_map.140 = (f32[3,64]{1,0:T(4,128)}, f32[48,7,8,256]{3,2,1,0:T(8,128)}, s32[1,128]{1,0:T(1,128)}) custom-call(f32[3,64]{1,0:T(4,128)} %refs_0_.1, f32[3,64]{1,0:T(4,128)} %refs_1_.1, s32[8,64]{1,0:T(8,128)} %refs_2_.1, s32[1,16]{1,0:T(1,128)} %bitcast.3, f32[3,8,64]{2,1,0:T(8,128)} %refs_4_.1, f32[1,64]{1,0:T(1,128)} %bitcast.4, f32[2,64]{1,0:T(2,128)} %refs_6_.1, ...), custom_call_target="tpu_custom_call" | custom-call | flops 7247757312 | bytes 11010048 | tf_op jit(solution)/shard_map/pallas_call | solution.py:804
  72.4 2.9 %shard_map.141 = (f32[3,64]{1,0:T(4,128)}, f32[7,24,8,256]{3,2,1,0:T(8,128)}) custom-call(s32[1,128]{1,0:T(1,128)} %get-tuple-element.5.order_hbm, f32[48,7,8,256]{3,2,1,0:T(8,128)} %get-tuple-element.6.got, f32[3,64]{1,0:T(4,128)} %get-tuple-element.7.residual), custom_call_target="tpu_custom_call" | custom-call | tf_op jit(solution)/shard_map/pallas_call | solution.py:897

commit v7 on v6

--- a/solution.py
+++ b/solution.py
@@ -358,6 +358,23 @@
         line = jnp.where(2 * line < planes, planes - 1 - ring, ring)
         return line * block + (lane + step) % block
 
+    pltpu.make_async_copy(state_hbm, st, load_sem.at[3]).start()
+    barrier = pltpu.get_barrier_semaphore()
+    total = groups * ranks
+    flat = me * ranks + mine
+
+    def greet(k, carry):
+        other = (flat + 1 + (k + total // 2) % (total - 1)) % total
+        pl.semaphore_signal(
+            barrier,
+            inc=1,
+            device_id={"macro": other // ranks, "vox": other % ranks},
+            device_id_type=pl.DeviceIdType.MESH,
+        )
+        return carry
+
+    lax.fori_loop(0, total - 1, greet, 0)
+
     fetches = {}
     for n, (src, dst) in enumerate(
         (
@@ -376,23 +393,9 @@
         )
     ):
         fetches[n] = pltpu.make_async_copy(src, dst, load_sem.at[n])
-        fetches[n].start()
-
-    barrier = pltpu.get_barrier_semaphore()
-    total = groups * ranks
-    flat = me * ranks + mine
-
-    def greet(k, carry):
-        other = (flat + k) % total
-        pl.semaphore_signal(
-            barrier,
-            inc=1,
-            device_id={"macro": other // ranks, "vox": other % ranks},
-            device_id_type=pl.DeviceIdType.MESH,
-        )
-        return carry
-
-    lax.fori_loop(1, total, greet, 0)
+        if n != 3:
+            fetches[n].start()
+
 
     rows_i[...] = jnp.full(rows_i.shape, -1, jnp.int32)
     fetches[0].wait()
@@ -627,9 +630,7 @@
                 send_row(low + 1, far)
 
     def third_hook(step):
-        @pl.when(step < SWEEPS // 2)
-        def _():
-            send_new(half * step, half * step + half, near)
+        pl.when(step < SWEEPS - 1)(lambda: send_new(2 * step + 2, 2 * step + 4, near))
 
     strain = strain_of(ranks * count_up((rows, LANES), 0) + mine)
     if ranks > 1:
@@ -681,6 +682,7 @@
         give_back(raw_new, 0, rows, groups, R_GOT + 1, 1, 0)
         if levels > 2:
             send_new(half, rows, far)
+            send_new(0, 2, near)
         else:
             send_new(0, rows, range(ranks))
     if levels > 2:

time: 75.5 us -> 75.8 us (level)
  no operation moved by 1% of the time
where the time goes in v7:
time: 75.8 us; the launch traced here: 75.6 us
  Pallas kernels  75 us (99%)
    pallas_call x1, Pallas kernels, exchange(): pl.pallas_call(functools.partial(exchange_kernel, levels), out_shape=[jax...  72.1 us
    pallas_call x1, Pallas kernels, pick_rows(): pl.pallas_call(pick_kernel, out_shape=[jax.ShapeDtypeStruct(residual.shap...  2.87 us

profile of v7, /device:TPU:0, one launch (start us, length us, event | category | flops | bytes accessed | tf_op | source)
XLA Modules:
  0.0 75.6 jit_solution(13418622808703082832)
XLA Ops:
  0.6 72.1 %shard_map.140 = (f32[3,64]{1,0:T(4,128)}, f32[48,7,8,256]{3,2,1,0:T(8,128)}, s32[1,128]{1,0:T(1,128)}) custom-call(f32[3,64]{1,0:T(4,128)} %refs_0_.1, f32[3,64]{1,0:T(4,128)} %refs_1_.1, s32[8,64]{1,0:T(8,128)} %refs_2_.1, s32[1,16]{1,0:T(1,128)} %bitcast.3, f32[3,8,64]{2,1,0:T(8,128)} %refs_4_.1, f32[1,64]{1,0:T(1,128)} %bitcast.4, f32[2,64]{1,0:T(2,128)} %refs_6_.1, ...), custom_call_target="tpu_custom_call" | custom-call | flops 7247757312 | bytes 11010048 | tf_op jit(solution)/shard_map/pallas_call | solution.py:806
  72.7 2.9 %shard_map.141 = (f32[3,64]{1,0:T(4,128)}, f32[7,24,8,256]{3,2,1,0:T(8,128)}) custom-call(s32[1,128]{1,0:T(1,128)} %get-tuple-element.5.order_hbm, f32[48,7,8,256]{3,2,1,0:T(8,128)} %get-tuple-element.6.got, f32[3,64]{1,0:T(4,128)} %get-tuple-element.7.residual), custom_call_target="tpu_custom_call" | custom-call | tf_op jit(solution)/shard_map/pallas_call | solution.py:899
